TPU v7x, 256 devices: a whole 4x4x8 slice. The times are simulated.
256 devices in a mesh: section: 16 (over y_hi, z), dp: 8 (over y_lo, x), mp: 2 (over core).
Axes of the slice: x: 4, y: 4 (y_hi: 2, y_lo: 2; y = y_hi * 2 + y_lo), z: 8, core: 2. Of those that a mesh axis runs over, the one named last changes fastest.
Arguments:
- old_w: float32 [16, 8, 16, 26, 3328], P(None, 'dp', 'section', None, 'mp'), may hold values from -0.109375 to 0.109375
- old_m: bfloat16 [16, 8, 16, 26, 3328], P(None, 'dp', 'section', None, 'mp'), may hold values from -12 to 12
- old_v: bfloat16 [16, 8, 16, 26, 3328], P(None, 'dp', 'section', None, 'mp'), may hold values from 0.5 to 20
- old_slot_layer: int32 [16], replicated, may hold values from 0 to 15, each once
- norm_gain: float32 [16, 3328], P('section'), may hold values from 0.5 to 2
- tokens: bfloat16 [8, 128, 3328], P(None, 'dp'), may hold values from -6 to 6
- cotangent: bfloat16 [8, 128, 3328], P(None, 'dp'), may hold values from -6 to 6
Outputs:
- new_w: float32 [16, 3328, 3328], P('section', 'dp', 'mp')
- new_m: bfloat16 [16, 3328, 3328], P('section', 'dp', 'mp')
- new_v: bfloat16 [16, 3328, 3328], P('section', 'dp', 'mp')
Inputs may be any that keep to these rules, and one draw needn't show every extreme that they name: `old_slot_layer`: every layer number appears exactly once.
All inputs are finite; a program needn't handle non-finite values.
Results may differ from a plain program's by a relative error of at most 0.028.
Values may be sent and summed in bfloat16 or wider, within the bound.
A program may use at most 128 MiB of HBM per device.

v0:
```python
import jax
import jax.numpy as jnp
from jax import lax
from jax.sharding import PartitionSpec as P

eps_norm = 1e-05
beta_one = 0.9
beta_two = 0.95
learn_rate = 0.001
decay_rate = 0.1
adam_eps = 1e-08
step_count = 1000.0


def from_behind(value, axis, by):
    count = lax.axis_size(axis)
    pairs = [(i, i + by) for i in range(count) if 0 <= i + by < count]
    return lax.ppermute(value, axis, pairs)


def silu_slope(values):
    sigmoid_value = jax.nn.sigmoid(values)
    return sigmoid_value * (1.0 + values * (1.0 - sigmoid_value))


def row_scale_of(inputs):
    widened = inputs.astype(jnp.float32)
    return lax.rsqrt(jnp.mean(widened * widened, axis=1, keepdims=True) + eps_norm)


def local(old_w, old_m, old_v, old_slot_layer, norm_gain, tokens, cotangent):
    sections = lax.axis_size("section")
    section_index = lax.axis_index("section")
    core_index = lax.axis_index("mp")
    micro_count = tokens.shape[0]
    row_count = tokens.shape[1]
    full_width = tokens.shape[2]
    piece_rows = old_w.shape[3]
    half_width = old_w.shape[4]
    row_block = sections * piece_rows
    token_total = micro_count * row_count
    ticks = micro_count + sections - 1
    layer_ids = jnp.arange(sections, dtype=jnp.int32)
    matches = (old_slot_layer[None, :] == layer_ids[:, None]).astype(jnp.int32)
    inverse = jnp.sum(matches * layer_ids[None, :], axis=1)
    ordered_w = jnp.take(old_w, inverse, axis=0)
    ordered_m = jnp.take(old_m, inverse, axis=0)
    ordered_v = jnp.take(old_v, inverse, axis=0)
    master = (
        lax.all_to_all(
            ordered_w.astype(jnp.bfloat16), "section", split_axis=0, concat_axis=2, tiled=True
        )
        .astype(ordered_w.dtype)
        .reshape(row_block, half_width)
    )
    moment_one, moment_two = (
        lax.all_to_all(ordered_m, "section", split_axis=0, concat_axis=2, tiled=True),
        lax.all_to_all(ordered_v, "section", split_axis=0, concat_axis=2, tiled=True),
    )
    moment_one = moment_one.reshape(row_block, half_width)
    moment_two = moment_two.reshape(row_block, half_width)
    weight_copy = lax.all_gather(master.astype(jnp.bfloat16), "dp", axis=0, tiled=True)
    gain_row = norm_gain[0]
    col_start = core_index * half_width

    def layer_forward(inputs):
        row_scale = row_scale_of(inputs)
        normed = (inputs.astype(jnp.float32) * row_scale * gain_row).astype(jnp.bfloat16)
        preact = jnp.dot(normed, weight_copy, preferred_element_type=jnp.float32)
        own_cols = lax.dynamic_slice_in_dim(inputs, col_start, half_width, 1).astype(jnp.float32)
        return ((own_cols + jax.nn.silu(preact)).astype(jnp.bfloat16), normed, preact)

    def forward_send(output):
        joined = lax.all_gather(output, "mp", axis=1, tiled=True)
        return from_behind(joined, "section", 1)

    def forward_tick(tick_index, loop_carry):
        arriving, stashed, normed_cols, preacts = loop_carry
        batch_index = tick_index - section_index
        active = (batch_index >= 0) & (batch_index < micro_count)
        slot_index = jnp.clip(batch_index, 0, micro_count - 1)
        entry_rows = lax.dynamic_index_in_dim(tokens, slot_index, 0, keepdims=False)
        inputs = jnp.where(section_index == 0, entry_rows, arriving)

        def forward_do_work(stash_state):
            stash_acts, stash_normed, stash_pre = stash_state
            output, normed, preact = layer_forward(inputs)
            stash_acts = lax.dynamic_update_index_in_dim(stash_acts, inputs, slot_index, 0)
            stash_normed = lax.dynamic_update_slice_in_dim(
                stash_normed, normed.T, slot_index * row_count, 1
            )
            stash_pre = lax.dynamic_update_index_in_dim(stash_pre, preact, slot_index, 0)
            return (output, (stash_acts, stash_normed, stash_pre))

        def skip_work(stash_state):
            return (jnp.zeros((row_count, half_width), jnp.bfloat16), stash_state)

        output, stash_state = lax.cond(
            active, forward_do_work, skip_work, (stashed, normed_cols, preacts)
        )
        arriving = forward_send(output)
        return (arriving,) + stash_state

    forward_init = (
        jnp.zeros((row_count, full_width), jnp.bfloat16),
        jnp.zeros((micro_count, row_count, full_width), jnp.bfloat16),
        jnp.zeros((full_width, token_total), jnp.bfloat16),
        jnp.zeros((micro_count, row_count, half_width), jnp.float32),
    )
    _, stashed, normed_cols, preacts = lax.fori_loop(0, ticks, forward_tick, forward_init)

    def grad_part(own_grad, slot_index, dpre_rows):
        preact = lax.dynamic_index_in_dim(preacts, slot_index, 0, keepdims=False)
        dpre = (own_grad.astype(jnp.float32) * silu_slope(preact)).astype(jnp.bfloat16)
        partial_value = lax.dot_general(
            dpre, weight_copy, (((1,), (1,)), ((), ())), preferred_element_type=jnp.float32
        )
        dpre_rows = lax.dynamic_update_slice_in_dim(dpre_rows, dpre, slot_index * row_count, 0)
        return (partial_value, dpre_rows)

    def skip_part(dpre_rows):
        return (jnp.zeros((row_count, full_width), jnp.float32), dpre_rows)

    dpre_init = jnp.zeros((token_total, half_width), jnp.bfloat16)

    def backward_tick(tick_index, loop_carry):
        arriving, dpre_rows = loop_carry
        batch_index = tick_index - (sections - 1 - section_index)
        active = (batch_index >= 0) & (batch_index < micro_count)
        slot_index = jnp.clip(batch_index, 0, micro_count - 1)
        seed_grad = lax.dynamic_index_in_dim(cotangent, slot_index, 0, keepdims=False)
        upstream = jnp.where(section_index == sections - 1, seed_grad, arriving)
        own_grad = lax.dynamic_slice_in_dim(upstream, col_start, half_width, 1)

        def backward_do_work(rows_state):
            return grad_part(own_grad, slot_index, rows_state)

        partial_value, dpre_rows = lax.cond(active, backward_do_work, skip_part, dpre_rows)
        summed = lax.psum(partial_value.astype(jnp.bfloat16), "mp").astype(jnp.float32)
        inputs = lax.dynamic_index_in_dim(stashed, slot_index, 0, keepdims=False)
        widened = inputs.astype(jnp.float32)
        row_scale = row_scale_of(inputs)
        weighted = gain_row * summed
        row_stat = jnp.mean(widened * weighted, axis=1, keepdims=True)
        cube = row_scale * row_scale * row_scale
        back_grad = (
            upstream.astype(jnp.float32) + row_scale * weighted - widened * cube * row_stat
        ).astype(jnp.bfloat16)
        arriving = from_behind(back_grad, "section", -1)
        return (arriving, dpre_rows)

    backward_init = (jnp.zeros((row_count, full_width), jnp.bfloat16), dpre_init)
    _, dpre_rows = lax.fori_loop(0, ticks, backward_tick, backward_init)
    features = lax.all_to_all(normed_cols, "dp", split_axis=0, concat_axis=1, tiled=True)
    weight_grad = jnp.dot(
        features,
        lax.all_gather(dpre_rows, "dp", axis=0, tiled=True),
        preferred_element_type=jnp.float32,
    )
    moment_next = beta_one * moment_one.astype(jnp.float32) + (1.0 - beta_one) * weight_grad
    second_next = (
        beta_two * moment_two.astype(jnp.float32) + (1.0 - beta_two) * weight_grad * weight_grad
    )
    fix_one = 1.0 - beta_one**step_count
    fix_two = 1.0 - beta_two**step_count
    direction = moment_next / fix_one / (jnp.sqrt(second_next / fix_two) + adam_eps)
    updated = master - learn_rate * (direction + decay_rate * master)
    return (
        updated[None],
        moment_next.astype(jnp.bfloat16)[None],
        second_next.astype(jnp.bfloat16)[None],
    )


def solution(mesh):
    placed = (
        P(None, "dp", "section", None, "mp"),
        P(None, "dp", "section", None, "mp"),
        P(None, "dp", "section", None, "mp"),
        P(),
        P("section", None),
        P(None, "dp", None),
        P(None, "dp", None),
    )
    return jax.shard_map(
        local,
        mesh=mesh,
        in_specs=placed,
        out_specs=(P("section", "dp", "mp"), P("section", "dp", "mp"), P("section", "dp", "mp")),
        check_vma=False,
    )
```

profile of v0, /device:TPU:1, one launch (start us, length us, event | category | flops | bytes accessed | tf_op | source)
XLA Modules:
  0.0 1792.4 jit_solution(4458749482543873117)
XLA Ops:
  11.6 52.9 %all_to_all.49 = bf16[16,1,1,26,1664]{4,3,2,1,0:T(8,128)(2,1)S(1)} all-to-all(bf16[16,1,1,26,1664]{4,3,2,1,0:T(8,128)(2,1)S(1)} %copy.45), channel_id=1, replica_groups=mesh['section'=16,'dp'=8,'mp'=2] {'section'}, dimensions={0} | all-to-all | bytes 2768896 | tf_op jit(solution)/shard_map/all_to_all | solution.py:50
  82.0 117.1 %all-gather.3.cloned.1.call-done = bf16[3328,1664]{1,0:T(8,128)(2,1)} async-done(((bf16[416,1664]{1,0:T(8,128)(2,1)}), bf16[3328,1664]{1,0:T(8,128)(2,1)}) %all-gather.3.cloned.1.call-update) | async-done | bytes 11075600 | tf_op jit(solution)/shard_map/all_gather | solution.py:62
  201.2 346.2 %while.40 = (s32[]{:T(128)}, bf16[16,3328]{1,0:T(8,128)(2,1)S(1)}, bf16[8,16,3328]{2,1,0:T(8,128)(2,1)S(1)}, bf16[3328,128]{0,1:T(8,128)(2,1)}, f32[8,16,1664]{2...) while((s32[]{:T(128)}, bf16[16,3328]{1,0:T(8,128)(2,1)S(1)}, ...), condition=%wide.region_5.7_spmd, body=%wide.region_1.6_spmd.sunk | while | flops 178034704 | bytes 12996824 | solution.py:110
  201.2 8.3 conditional.4
  215.5 8.3 conditional.4
  232.2 8.3 conditional.4
  249.3 8.3 conditional.4
  266.4 8.3 conditional.4
  283.4 8.3 conditional.4
  300.5 8.3 conditional.4
  317.5 8.3 conditional.4
  337.3 12.4 collective-permute-start
  363.2 10.6 collective-permute-start
  388.5 13.6 collective-permute-start
  416.8 13.6 collective-permute-start
  445.0 9.0 collective-permute-start
  468.7 10.6 collective-permute-start
  496.4 16.0 collective-permute-start
  529.4 16.0 collective-permute-start
  547.4 1156.1 %while.41 = (s32[]{:T(128)}, bf16[16,3328]{1,0:T(8,128)(2,1)S(1)}, bf16[128,1664]{1,0:T(8,128)(2,1)S(1)}, pred[]{:T(512)}, s32[]{:T(128)}, /*index=5*/bf16[8,16,...) while((s32[]{:T(128)}, bf16[16,3328]{1,0:T(8,128)(2,1)S(1)}, ...), condition=%wide.region_12.14_spmd, body=%wide.region_6.13_spmd.sunk | while | flops 178753584 | bytes 14059120 | solution.py:153
  549.2 94.5 %all-reduce.2.cloned.1.call-done = bf16[16,3328]{1,0:T(8,128)(2,1)} async-done(((bf16[16,3328]{1,0:T(8,128)(2,1)}), bf16[16,3328]{1,0:T(8,128)(2,1)}) %all-reduce.2.cloned.1.call-update) | async-done | bytes 106512 | tf_op jit(solution)/shard_map/while/body/eval_jaxpr/psum | solution.py:139
  653.6 37.5 %all-reduce.2.cloned.1.call-done = bf16[16,3328]{1,0:T(8,128)(2,1)} async-done(((bf16[16,3328]{1,0:T(8,128)(2,1)}), bf16[16,3328]{1,0:T(8,128)(2,1)}) %all-reduce.2.cloned.1.call-update) | async-done | bytes 106512 | tf_op jit(solution)/shard_map/while/body/eval_jaxpr/psum | solution.py:139
  701.0 38.3 %all-reduce.2.cloned.1.call-done = bf16[16,3328]{1,0:T(8,128)(2,1)} async-done(((bf16[16,3328]{1,0:T(8,128)(2,1)}), bf16[16,3328]{1,0:T(8,128)(2,1)}) %all-reduce.2.cloned.1.call-update) | async-done | bytes 106512 | tf_op jit(solution)/shard_map/while/body/eval_jaxpr/psum | solution.py:139
  749.3 39.2 %all-reduce.2.cloned.1.call-done = bf16[16,3328]{1,0:T(8,128)(2,1)} async-done(((bf16[16,3328]{1,0:T(8,128)(2,1)}), bf16[16,3328]{1,0:T(8,128)(2,1)}) %all-reduce.2.cloned.1.call-update) | async-done | bytes 106512 | tf_op jit(solution)/shard_map/while/body/eval_jaxpr/psum | solution.py:139
  798.4 39.2 %all-reduce.2.cloned.1.call-done = bf16[16,3328]{1,0:T(8,128)(2,1)} async-done(((bf16[16,3328]{1,0:T(8,128)(2,1)}), bf16[16,3328]{1,0:T(8,128)(2,1)}) %all-reduce.2.cloned.1.call-update) | async-done | bytes 106512 | tf_op jit(solution)/shard_map/while/body/eval_jaxpr/psum | solution.py:139
  847.5 39.2 %all-reduce.2.cloned.1.call-done = bf16[16,3328]{1,0:T(8,128)(2,1)} async-done(((bf16[16,3328]{1,0:T(8,128)(2,1)}), bf16[16,3328]{1,0:T(8,128)(2,1)}) %all-reduce.2.cloned.1.call-update) | async-done | bytes 106512 | tf_op jit(solution)/shard_map/while/body/eval_jaxpr/psum | solution.py:139
  896.6 39.2 %all-reduce.2.cloned.1.call-done = bf16[16,3328]{1,0:T(8,128)(2,1)} async-done(((bf16[16,3328]{1,0:T(8,128)(2,1)}), bf16[16,3328]{1,0:T(8,128)(2,1)}) %all-reduce.2.cloned.1.call-update) | async-done | bytes 106512 | tf_op jit(solution)/shard_map/while/body/eval_jaxpr/psum | solution.py:139
  945.7 39.2 %all-reduce.2.cloned.1.call-done = bf16[16,3328]{1,0:T(8,128)(2,1)} async-done(((bf16[16,3328]{1,0:T(8,128)(2,1)}), bf16[16,3328]{1,0:T(8,128)(2,1)}) %all-reduce.2.cloned.1.call-update) | async-done | bytes 106512 | tf_op jit(solution)/shard_map/while/body/eval_jaxpr/psum | solution.py:139
  994.8 39.2 %all-reduce.2.cloned.1.call-done = bf16[16,3328]{1,0:T(8,128)(2,1)} async-done(((bf16[16,3328]{1,0:T(8,128)(2,1)}), bf16[16,3328]{1,0:T(8,128)(2,1)}) %all-reduce.2.cloned.1.call-update) | async-done | bytes 106512 | tf_op jit(solution)/shard_map/while/body/eval_jaxpr/psum | solution.py:139
  1043.9 39.2 %all-reduce.2.cloned.1.call-done = bf16[16,3328]{1,0:T(8,128)(2,1)} async-done(((bf16[16,3328]{1,0:T(8,128)(2,1)}), bf16[16,3328]{1,0:T(8,128)(2,1)}) %all-reduce.2.cloned.1.call-update) | async-done | bytes 106512 | tf_op jit(solution)/shard_map/while/body/eval_jaxpr/psum | solution.py:139
  1093.0 39.2 %all-reduce.2.cloned.1.call-done = bf16[16,3328]{1,0:T(8,128)(2,1)} async-done(((bf16[16,3328]{1,0:T(8,128)(2,1)}), bf16[16,3328]{1,0:T(8,128)(2,1)}) %all-reduce.2.cloned.1.call-update) | async-done | bytes 106512 | tf_op jit(solution)/shard_map/while/body/eval_jaxpr/psum | solution.py:139
  1142.1 38.8 %all-reduce.2.cloned.1.call-done = bf16[16,3328]{1,0:T(8,128)(2,1)} async-done(((bf16[16,3328]{1,0:T(8,128)(2,1)}), bf16[16,3328]{1,0:T(8,128)(2,1)}) %all-reduce.2.cloned.1.call-update) | async-done | bytes 106512 | tf_op jit(solution)/shard_map/while/body/eval_jaxpr/psum | solution.py:139
  1190.8 38.8 %all-reduce.2.cloned.1.call-done = bf16[16,3328]{1,0:T(8,128)(2,1)} async-done(((bf16[16,3328]{1,0:T(8,128)(2,1)}), bf16[16,3328]{1,0:T(8,128)(2,1)}) %all-reduce.2.cloned.1.call-update) | async-done | bytes 106512 | tf_op jit(solution)/shard_map/while/body/eval_jaxpr/psum | solution.py:139
  1239.6 38.8 %all-reduce.2.cloned.1.call-done = bf16[16,3328]{1,0:T(8,128)(2,1)} async-done(((bf16[16,3328]{1,0:T(8,128)(2,1)}), bf16[16,3328]{1,0:T(8,128)(2,1)}) %all-reduce.2.cloned.1.call-update) | async-done | bytes 106512 | tf_op jit(solution)/shard_map/while/body/eval_jaxpr/psum | solution.py:139
  1288.3 38.8 %all-reduce.2.cloned.1.call-done = bf16[16,3328]{1,0:T(8,128)(2,1)} async-done(((bf16[16,3328]{1,0:T(8,128)(2,1)}), bf16[16,3328]{1,0:T(8,128)(2,1)}) %all-reduce.2.cloned.1.call-update) | async-done | bytes 106512 | tf_op jit(solution)/shard_map/while/body/eval_jaxpr/psum | solution.py:139
  1336.3 8.2 conditional.5
  1345.3 30.6 %all-reduce.2.cloned.1.call-done = bf16[16,3328]{1,0:T(8,128)(2,1)} async-done(((bf16[16,3328]{1,0:T(8,128)(2,1)}), bf16[16,3328]{1,0:T(8,128)(2,1)}) %all-reduce.2.cloned.1.call-update) | async-done | bytes 106512 | tf_op jit(solution)/shard_map/while/body/eval_jaxpr/psum | solution.py:139
  1385.1 8.2 conditional.5
  1394.0 29.4 %all-reduce.2.cloned.1.call-done = bf16[16,3328]{1,0:T(8,128)(2,1)} async-done(((bf16[16,3328]{1,0:T(8,128)(2,1)}), bf16[16,3328]{1,0:T(8,128)(2,1)}) %all-reduce.2.cloned.1.call-update) | async-done | bytes 106512 | tf_op jit(solution)/shard_map/while/body/eval_jaxpr/psum | solution.py:139
  1441.6 29.4 %all-reduce.2.cloned.1.call-done = bf16[16,3328]{1,0:T(8,128)(2,1)} async-done(((bf16[16,3328]{1,0:T(8,128)(2,1)}), bf16[16,3328]{1,0:T(8,128)(2,1)}) %all-reduce.2.cloned.1.call-update) | async-done | bytes 106512 | tf_op jit(solution)/shard_map/while/body/eval_jaxpr/psum | solution.py:139
  1489.1 29.4 %all-reduce.2.cloned.1.call-done = bf16[16,3328]{1,0:T(8,128)(2,1)} async-done(((bf16[16,3328]{1,0:T(8,128)(2,1)}), bf16[16,3328]{1,0:T(8,128)(2,1)}) %all-reduce.2.cloned.1.call-update) | async-done | bytes 106512 | tf_op jit(solution)/shard_map/while/body/eval_jaxpr/psum | solution.py:139
  1536.7 28.4 %all-reduce.2.cloned.1.call-done = bf16[16,3328]{1,0:T(8,128)(2,1)} async-done(((bf16[16,3328]{1,0:T(8,128)(2,1)}), bf16[16,3328]{1,0:T(8,128)(2,1)}) %all-reduce.2.cloned.1.call-update) | async-done | bytes 106512 | tf_op jit(solution)/shard_map/while/body/eval_jaxpr/psum | solution.py:139
  1583.2 26.2 %all-reduce.2.cloned.1.call-done = bf16[16,3328]{1,0:T(8,128)(2,1)} async-done(((bf16[16,3328]{1,0:T(8,128)(2,1)}), bf16[16,3328]{1,0:T(8,128)(2,1)}) %all-reduce.2.cloned.1.call-update) | async-done | bytes 106512 | tf_op jit(solution)/shard_map/while/body/eval_jaxpr/psum | solution.py:139
  1627.6 25.2 %all-reduce.2.cloned.1.call-done = bf16[16,3328]{1,0:T(8,128)(2,1)} async-done(((bf16[16,3328]{1,0:T(8,128)(2,1)}), bf16[16,3328]{1,0:T(8,128)(2,1)}) %all-reduce.2.cloned.1.call-update) | async-done | bytes 106512 | tf_op jit(solution)/shard_map/while/body/eval_jaxpr/psum | solution.py:139
  1671.0 24.3 %all-reduce.2.cloned.1.call-done = bf16[16,3328]{1,0:T(8,128)(2,1)} async-done(((bf16[16,3328]{1,0:T(8,128)(2,1)}), bf16[16,3328]{1,0:T(8,128)(2,1)}) %all-reduce.2.cloned.1.call-update) | async-done | bytes 106512 | tf_op jit(solution)/shard_map/while/body/eval_jaxpr/psum | solution.py:139
  1704.4 9.1 all-to-all-start.3
  1714.7 41.8 %all-to-all-done.3 = bf16[16,1,1,26,1664]{4,3,2,1,0:T(8,128)(2,1)} async-done(((bf16[16,1,1,26,1664]{4,3,2,1,0:T(8,128)(2,1)}), bf16[16,1,1,26,1664]{4,3,2,1,0:T(8,128)(2,1)}, u32[]{:S(2)}, u32[]{:S(2)}) %all-to-all-start.3) | async-done | bytes 1384480 | tf_op jit(solution)/shard_map/all_to_all | solution.py:58
  1776.2 9.6 convert_bitcast_fusion
  (498 shorter events, 632.1 us)
Async XLA Ops:
  7.2 192.0 %all-gather.3.cloned.1.call-start = ((), (), s32[]{:S(2)}) async-start(), calls=%async_computation.4 | async-start | bytes 12460032 | tf_op jit(solution)/shard_map/all_gather | solution.py:62
  76.5 1627.8 %all-to-all-start.1 = ((bf16[16,1,1,26,1664]{4,3,2,1,0:T(8,128)(2,1)}), bf16[16,1,1,26,1664]{4,3,2,1,0:T(8,128)(2,1)S(1)}, u32[]{:S(2)}, u32[]{:S(2)}) async-start(bf16[16,1,1,26,1664]{4,3,2,1,0:T(8,128)(2,1)} %get-tuple-element.689), calls=%async_computation.1 | async-start | bytes 3407872 | tf_op jit(solution)/shard_map/all_to_all | solution.py:57
  337.3 14.3 collective-permute-start
  363.2 12.6 collective-permute-start
  378.5 7.3 collective-permute-start
  388.5 15.5 collective-permute-start
  406.8 7.3 collective-permute-start
  416.8 15.5 collective-permute-start
  435.0 7.3 collective-permute-start
  445.0 10.9 collective-permute-start
  458.7 7.3 collective-permute-start
  468.7 12.5 collective-permute-start
  484.0 9.7 collective-permute-start
  496.4 17.9 %collective-permute-start = (bf16[16,3328]{1,0:T(8,128)(2,1)S(1)}, bf16[16,3328]{1,0:T(8,128)(2,1)S(1)}, u32[]{:S(2)}, u32[]{:S(2)}) collective-permute-start(bf16[16,3328]{1,0:T(8,128)(2,1)S(1)} %all_gather.17), channel_id=1, source_target_pairs={{0,16},{16,32},{32,48},{48,64},{64,80},{80,96},{96,112},{112,128},... | collective-permute-start | bytes 319496 | tf_op jit(solution)/shard_map/while/body/eval_jaxpr/ppermute | solution.py:18
  517.0 9.7 collective-permute-start
  529.4 17.9 %collective-permute-start = (bf16[16,3328]{1,0:T(8,128)(2,1)S(1)}, bf16[16,3328]{1,0:T(8,128)(2,1)S(1)}, u32[]{:S(2)}, u32[]{:S(2)}) collective-permute-start(bf16[16,3328]{1,0:T(8,128)(2,1)S(1)} %all_gather.17), channel_id=1, source_target_pairs={{0,16},{16,32},{32,48},{48,64},{64,80},{80,96},{96,112},{112,128},... | collective-permute-start | bytes 319496 | tf_op jit(solution)/shard_map/while/body/eval_jaxpr/ppermute | solution.py:18
  547.4 96.2 %all-reduce.2.cloned.1.call-start = ((), (), s32[]{:S(2)}) async-start(), calls=%async_computation.6 | async-start | bytes 212992 | tf_op jit(solution)/shard_map/while/body/eval_jaxpr/psum | solution.py:139
  651.9 39.2 %all-reduce.2.cloned.1.call-start = ((), (), s32[]{:S(2)}) async-start(), calls=%async_computation.6 | async-start | bytes 212992 | tf_op jit(solution)/shard_map/while/body/eval_jaxpr/psum | solution.py:139
  693.2 6.2 collective-permute-start.1
  699.4 40.0 %all-reduce.2.cloned.1.call-start = ((), (), s32[]{:S(2)}) async-start(), calls=%async_computation.6 | async-start | bytes 212992 | tf_op jit(solution)/shard_map/while/body/eval_jaxpr/psum | solution.py:139
  747.6 40.8 %all-reduce.2.cloned.1.call-start = ((), (), s32[]{:S(2)}) async-start(), calls=%async_computation.6 | async-start | bytes 212992 | tf_op jit(solution)/shard_map/while/body/eval_jaxpr/psum | solution.py:139
  790.6 6.2 collective-permute-start.1
  796.7 40.8 %all-reduce.2.cloned.1.call-start = ((), (), s32[]{:S(2)}) async-start(), calls=%async_computation.6 | async-start | bytes 212992 | tf_op jit(solution)/shard_map/while/body/eval_jaxpr/psum | solution.py:139
  839.7 6.2 collective-permute-start.1
  845.8 40.8 %all-reduce.2.cloned.1.call-start = ((), (), s32[]{:S(2)}) async-start(), calls=%async_computation.6 | async-start | bytes 212992 | tf_op jit(solution)/shard_map/while/body/eval_jaxpr/psum | solution.py:139
  894.9 40.8 %all-reduce.2.cloned.1.call-start = ((), (), s32[]{:S(2)}) async-start(), calls=%async_computation.6 | async-start | bytes 212992 | tf_op jit(solution)/shard_map/while/body/eval_jaxpr/psum | solution.py:139
  937.9 6.2 collective-permute-start.1
  944.0 40.8 %all-reduce.2.cloned.1.call-start = ((), (), s32[]{:S(2)}) async-start(), calls=%async_computation.6 | async-start | bytes 212992 | tf_op jit(solution)/shard_map/while/body/eval_jaxpr/psum | solution.py:139
  993.1 40.8 %all-reduce.2.cloned.1.call-start = ((), (), s32[]{:S(2)}) async-start(), calls=%async_computation.6 | async-start | bytes 212992 | tf_op jit(solution)/shard_map/while/body/eval_jaxpr/psum | solution.py:139
  1042.2 40.8 %all-reduce.2.cloned.1.call-start = ((), (), s32[]{:S(2)}) async-start(), calls=%async_computation.6 | async-start | bytes 212992 | tf_op jit(solution)/shard_map/while/body/eval_jaxpr/psum | solution.py:139
  1091.3 40.8 %all-reduce.2.cloned.1.call-start = ((), (), s32[]{:S(2)}) async-start(), calls=%async_computation.6 | async-start | bytes 212992 | tf_op jit(solution)/shard_map/while/body/eval_jaxpr/psum | solution.py:139
  1140.4 40.5 %all-reduce.2.cloned.1.call-start = ((), (), s32[]{:S(2)}) async-start(), calls=%async_computation.6 | async-start | bytes 212992 | tf_op jit(solution)/shard_map/while/body/eval_jaxpr/psum | solution.py:139
  1183.0 6.2 collective-permute-start.1
  1189.2 40.5 %all-reduce.2.cloned.1.call-start = ((), (), s32[]{:S(2)}) async-start(), calls=%async_computation.6 | async-start | bytes 212992 | tf_op jit(solution)/shard_map/while/body/eval_jaxpr/psum | solution.py:139
  1237.9 40.5 %all-reduce.2.cloned.1.call-start = ((), (), s32[]{:S(2)}) async-start(), calls=%async_computation.6 | async-start | bytes 212992 | tf_op jit(solution)/shard_map/while/body/eval_jaxpr/psum | solution.py:139
  1286.7 40.5 %all-reduce.2.cloned.1.call-start = ((), (), s32[]{:S(2)}) async-start(), calls=%async_computation.6 | async-start | bytes 212992 | tf_op jit(solution)/shard_map/while/body/eval_jaxpr/psum | solution.py:139
  1329.2 6.2 collective-permute-start.1
  1335.4 40.5 %all-reduce.2.cloned.1.call-start = ((), (), s32[]{:S(2)}) async-start(), calls=%async_computation.6 | async-start | bytes 212992 | tf_op jit(solution)/shard_map/while/body/eval_jaxpr/psum | solution.py:139
  1384.1 39.3 %all-reduce.2.cloned.1.call-start = ((), (), s32[]{:S(2)}) async-start(), calls=%async_computation.6 | async-start | bytes 212992 | tf_op jit(solution)/shard_map/while/body/eval_jaxpr/psum | solution.py:139
  1431.7 39.3 %all-reduce.2.cloned.1.call-start = ((), (), s32[]{:S(2)}) async-start(), calls=%async_computation.6 | async-start | bytes 212992 | tf_op jit(solution)/shard_map/while/body/eval_jaxpr/psum | solution.py:139
  1479.2 39.3 %all-reduce.2.cloned.1.call-start = ((), (), s32[]{:S(2)}) async-start(), calls=%async_computation.6 | async-start | bytes 212992 | tf_op jit(solution)/shard_map/while/body/eval_jaxpr/psum | solution.py:139
  1526.8 38.3 %all-reduce.2.cloned.1.call-start = ((), (), s32[]{:S(2)}) async-start(), calls=%async_computation.6 | async-start | bytes 212992 | tf_op jit(solution)/shard_map/while/body/eval_jaxpr/psum | solution.py:139
  1573.4 36.1 %all-reduce.2.cloned.1.call-start = ((), (), s32[]{:S(2)}) async-start(), calls=%async_computation.6 | async-start | bytes 212992 | tf_op jit(solution)/shard_map/while/body/eval_jaxpr/psum | solution.py:139
  1617.8 35.1 %all-reduce.2.cloned.1.call-start = ((), (), s32[]{:S(2)}) async-start(), calls=%async_computation.6 | async-start | bytes 212992 | tf_op jit(solution)/shard_map/while/body/eval_jaxpr/psum | solution.py:139
  1661.1 34.1 %all-reduce.2.cloned.1.call-start = ((), (), s32[]{:S(2)}) async-start(), calls=%async_computation.6 | async-start | bytes 212992 | tf_op jit(solution)/shard_map/while/body/eval_jaxpr/psum | solution.py:139
  1703.5 72.7 %all-gather.5.cloned.1.call-start = ((), (), s32[]{:S(2)}) async-start(), calls=%async_computation.5 | async-start | bytes 3833856 | tf_op jit(solution)/shard_map/all_gather | solution.py:157
  1704.4 52.2 %all-to-all-start.3 = ((bf16[16,1,1,26,1664]{4,3,2,1,0:T(8,128)(2,1)}), bf16[16,1,1,26,1664]{4,3,2,1,0:T(8,128)(2,1)}, u32[]{:S(2)}, u32[]{:S(2)}) async-start(bf16[16,1,1,26,1664]{4,3,2,1,0:T(8,128)(2,1)} %get-tuple-element.688), calls=%async_computation.3 | async-start | bytes 3407872 | tf_op jit(solution)/shard_map/all_to_all | solution.py:58
  1756.5 19.7 %all-to-all-start.2 = ((bf16[8,416,128]{2,1,0:T(8,128)(2,1)}), bf16[8,416,128]{2,1,0:T(8,128)(2,1)}, u32[]{:S(2)}, u32[]{:S(2)}) async-start(bf16[8,416,128]{2,1,0:T(8,128)(2,1)} %bitcast.16), calls=%async_computation.2 | async-start | bytes 1703936 | tf_op jit(solution)/shard_map/all_to_all | solution.py:154
  (54 other events, 361.2 us)
Sparse Core Ops, SparseCore 0:
  65.9 133.1 all-gather.2
  550.8 92.7 all-reduce.1
  655.3 35.8 all-reduce.1
  702.4 36.9 all-reduce.1
  750.7 37.7 all-reduce.1
  799.8 37.7 all-reduce.1
  849.2 37.4 all-reduce.1
  898.3 37.4 all-reduce.1
  947.4 37.4 all-reduce.1
  996.2 37.7 all-reduce.1
  1045.6 37.4 all-reduce.1
  1094.4 37.7 all-reduce.1
  1143.8 37.0 all-reduce.1
  1192.2 37.3 all-reduce.1
  1240.9 37.3 all-reduce.1
  1289.7 37.3 all-reduce.1
  1345.3 30.4 all-reduce.1
  1394.1 29.3 all-reduce.1
  1441.6 29.2 all-reduce.1
  1489.2 29.3 all-reduce.1
  1536.8 28.3 all-reduce.1
  1583.3 26.1 all-reduce.1
  1627.7 25.1 all-reduce.1
  1671.1 24.1 all-reduce.1
  1706.1 61.7 all-gather.4
where the time goes:
time: 1810 us; the launch traced here: 1790 us
  waiting for transfers between devices  1190 us (66%)
  starting transfers between devices  221 us (12%)
  blocking collectives  115 us (6%)
  matrix products  113 us (6%)
  other arithmetic  101 us (6%)
  local copies, waits for them, and re-layouts  39.3 us (2%)
    psum x23, waiting for transfers between devices, backward_tick(): lax.psum(partial_value.astype(jnp.bfloat16), 'mp').astype(jnp.float32)  862 us
    ppermute x46, starting transfers between devices, from_behind(): return lax.ppermute(value, axis, pairs)  202 us
    ppermute x46, waiting for transfers between devices, from_behind(): return lax.ppermute(value, axis, pairs)  157 us
    all_gather x1, waiting for transfers between devices, local(): lax.all_gather(master.astype(jnp.bfloat16), 'dp', axis=0, tiled=True)  117 us
    all_gather x23, blocking collectives, forward_send(): joined = lax.all_gather(output, 'mp', axis=1, tiled=True)  62.1 us
    dot_general x8, matrix products, grad_part(): lax.dot_general(dpre, weight_copy, (((1,), (1,)), ((), ())), preferred_el...  57.5 us
    all_to_all x1, blocking collectives, local(): lax.all_to_all(ordered_w.astype(jnp.bfloat16), 'section', split_axis=0, c...  52.9 us
    dot_general x8, matrix products, layer_forward(): preact = jnp.dot(normed, weight_copy, preferred_element_type=jnp.float32)  45.9 us
  transfers between devices with their start and end apart: 74, of which 72 were waited for; matrix products, arithmetic and copies ran while one was open for 12% of the time, Pallas kernels for 0%

commit v1 on v0

v1 whole, which is shorter than its diff:
```python
import functools

import jax
import jax.numpy as jnp
from jax import lax
from jax.experimental import pallas as pl
from jax.experimental.pallas import tpu as pltpu
from jax.sharding import PartitionSpec as P

eps_norm = 1e-05
beta_one = 0.9
beta_two = 0.95
learn_rate = 0.001
decay_rate = 0.1
adam_eps = 1e-08
step_count = 1000.0

MESH = pl.DeviceIdType.MESH
F32 = jnp.float32
BF16 = jnp.bfloat16
XS = 4


def remote(src, dst, send_sem, recv_sem, device):
    return pltpu.make_async_remote_copy(
        src_ref=src,
        dst_ref=dst,
        send_sem=send_sem,
        recv_sem=recv_sem,
        device_id=device,
        device_id_type=MESH,
    )


def relay_plan(rows):
    two_thirds = max(16, (rows * 2 // 3 + 15) // 16 * 16)
    half = (rows // 2 + 15) // 16 * 16
    return two_thirds, half


def kernel(
    sizes,
    order,
    old_w,
    old_m,
    old_v,
    gain,
    tokens,
    cotangent,
    new_w,
    new_m,
    new_v,
    w_send,
    m_send,
    v_send,
    w_recv,
    m_recv,
    v_recv,
    wide,
    block,
    weights,
    acts,
    outs,
    preacts,
    scales,
    normed,
    normed_t,
    feats,
    grads_in,
    grads_out,
    dpres,
    part_send,
    part_recv,
    stat_send,
    stat_recv,
    ws,
    wr,
    ms,
    mr,
    vs,
    vr,
    gs,
    gr,
    fs,
    fr,
    rs,
    rr,
    ps,
    pr,
    ss,
    sr,
    bs,
    br,
    ts,
    tr,
    ds,
    dr,
    local_sem,
):
    S, D, pr_rows, H, MB, R = sizes
    RB = S * pr_rows
    TOK = MB * R
    E = 2 * H
    s = lax.axis_index("section")
    a = lax.axis_index("dp")
    c = lax.axis_index("mp")
    sib = {"mp": 1 - c}

    barrier = pltpu.get_barrier_semaphore()

    @pl.loop(1, S)
    def _(k):
        pl.semaphore_signal(
            barrier, inc=1, device_id={"section": lax.rem(s + k, S)}, device_id_type=MESH
        )

    @pl.loop(1, D)
    def _(k):
        pl.semaphore_signal(
            barrier, inc=1, device_id={"dp": lax.rem(a + k, D)}, device_id_type=MESH
        )

    pl.semaphore_signal(barrier, inc=1, device_id=sib, device_id_type=MESH)

    @pl.when(s == 0)
    def _():
        @pl.loop(0, MB)
        def _(b):
            pltpu.make_async_copy(
                tokens.at[b, :, pl.ds(pl.multiple_of(c * H, 128), H)],
                acts.at[b, c],
                local_sem.at[b],
            ).start()

    @pl.when(s == S - 1)
    def _():
        @pl.loop(0, MB)
        def _(b):
            pltpu.make_async_copy(
                cotangent.at[b, :, pl.ds(pl.multiple_of(c * H, 128), H)],
                grads_in.at[b],
                local_sem.at[MB + b],
            ).start()

    @pl.loop(0, S)
    def _(k):
        w_send[k] = old_w[order[k]].astype(BF16)

    @pl.loop(0, S)
    def _(k):
        m_send[k] = old_m[order[k]]
        v_send[k] = old_v[order[k]]

    pl.semaphore_wait(barrier, S + D - 1)

    def scatter(send, recv, send_sems, recv_sems):
        @pl.loop(1, S)
        def _(k):
            to = lax.rem(s + k, S)
            remote(
                send.at[to], recv.at[s], send_sems.at[to], recv_sems.at[s], {"section": to}
            ).start()

        recv[s] = send[s]

    def arrived(send, recv, send_sems, recv_sems):
        @pl.loop(1, S)
        def _(k):
            of = lax.rem(s + k, S)
            remote(
                send.at[of], recv.at[of], send_sems.at[of], recv_sems.at[of], {"section": of}
            ).wait_recv()

    def drained(send, recv, send_sems, recv_sems):
        @pl.loop(1, S)
        def _(k):
            of = lax.rem(s + k, S)
            remote(
                send.at[of], recv.at[of], send_sems.at[of], recv_sems.at[of], {"section": of}
            ).wait_send()

    def assemble(recv, dst):
        @pl.loop(0, H // 128)
        def _(j):
            cols = pl.ds(pl.multiple_of(j * 128, 128), 128)
            for b in range(S):
                wide[pr_rows * b : pr_rows * (b + 1), :] = recv[b, :, cols].astype(F32)
            dst[:, cols] = wide[...].astype(BF16)

    scatter(w_send, w_recv, ws, wr)
    arrived(w_send, w_recv, ws, wr)
    scatter(m_send, m_recv, ms, mr)
    scatter(v_send, v_recv, vs, vr)
    assemble(w_recv, block)

    def rows_of(owner, r0, n):
        return weights.at[pl.ds(pl.multiple_of(owner * RB + r0, 16), n), :]

    own_copy = pltpu.make_async_copy(block, rows_of(a, 0, RB), local_sem.at[2 * MB])
    own_copy.start()
    pending = []
    if D == 2 * XS:
        x = lax.rem(a, XS)
        h = a // XS

        def at(dx, dh):
            hh = (1 - h) if dh else h
            return hh * XS + lax.rem(x + dx + XS, XS)

        third, half = relay_plan(RB)
        UP, DOWN, ACROSS = at(1, 0), at(-1, 0), at(0, 1)

        def start(sem, src, owner, r0, n, to):
            cp = remote(
                src, rows_of(owner, r0, n), gs.at[sem], gr.at[sem], {"dp": to}
            )
            cp.start()
            pending.append(cp)

        def relay(sem, owner, r0, n, to):
            start(sem, rows_of(owner, r0, n), owner, r0, n, to)

        def landed(sem, owner, r0, n):
            pltpu.make_async_copy(
                rows_of(owner, r0, n), rows_of(owner, r0, n), gr.at[sem]
            ).wait()

        def blk(r0, n):
            return block.at[pl.ds(r0, n), :]

        start(0, blk(third, RB - third), a, third, RB - third, ACROSS)
        start(1, blk(0, third), a, 0, third, ACROSS)
        start(2, blk(0, half), a, 0, half, UP)
        start(3, blk(half, RB - half), a, half, RB - half, DOWN)
        start(4, blk(half, RB - half), a, half, RB - half, UP)
        start(5, blk(0, half), a, 0, half, DOWN)
        landed(0, ACROSS, third, RB - third)
        relay(6, ACROSS, third, RB - third, UP)
        relay(7, ACROSS, third, RB - third, DOWN)
        landed(2, DOWN, 0, half)
        relay(8, DOWN, 0, half, UP)
        landed(3, UP, half, RB - half)
        relay(9, UP, half, RB - half, DOWN)
        landed(4, DOWN, half, RB - half)
        landed(5, UP, 0, half)
        relay(10, DOWN, 0, third, ACROSS)
        relay(11, UP, 0, third, ACROSS)
        landed(1, ACROSS, 0, third)
        landed(6, at(-1, 1), third, RB - third)
        landed(7, at(1, 1), third, RB - third)
        landed(10, at(-1, 1), 0, third)
        relay(12, at(-1, 1), 0, half, UP)
        landed(11, at(1, 1), 0, third)
        relay(13, at(1, 1), half, RB - half, DOWN)
        landed(8, at(2, 0), 0, half)
        landed(9, at(2, 0), half, RB - half)
        landed(12, at(2, 1), 0, half)
        landed(13, at(2, 1), half, RB - half)
    else:
        for k in range(1, D):
            to = lax.rem(a + k, D)
            cp = remote(block, rows_of(a, 0, RB), gs.at[k], gr.at[k], {"dp": to})
            cp.start()
            pending.append(cp)
        for k in range(1, D):
            of = lax.rem(a - k + D, D)
            pltpu.make_async_copy(rows_of(of, 0, RB), rows_of(of, 0, RB), gr.at[k]).wait()
    own_copy.wait()

    own_rows = pl.ds(pl.multiple_of(c * H, 128), H)
    sib_rows = pl.ds(pl.multiple_of((1 - c) * H, 128), H)
    gain_own = gain[c]
    gain_sib = gain[1 - c]

    @pl.loop(0, MB)
    def _(b):
        @pl.when(s == 0)
        def _():
            pltpu.make_async_copy(
                tokens.at[b, :, pl.ds(pl.multiple_of(c * H, 128), H)],
                acts.at[b, c],
                local_sem.at[b],
            ).wait()

        @pl.when(s > 0)
        def _():
            pltpu.make_async_copy(outs.at[b], acts.at[b, c], fr.at[b]).wait()

        remote(acts.at[b, c], acts.at[b, c], rs.at[b], rr.at[b], sib).start()
        x_own = acts[b, c].astype(F32)
        square = jnp.sum(x_own * x_own, axis=1, keepdims=True)
        total = jnp.dot(
            (x_own * gain_own).astype(BF16), weights[own_rows, :], preferred_element_type=F32
        )
        pltpu.make_async_copy(acts.at[b, 1 - c], acts.at[b, 1 - c], rr.at[b]).wait()
        x_sib = acts[b, 1 - c].astype(F32)
        square = square + jnp.sum(x_sib * x_sib, axis=1, keepdims=True)
        total = total + jnp.dot(
            (x_sib * gain_sib).astype(BF16), weights[sib_rows, :], preferred_element_type=F32
        )
        scale = lax.rsqrt(square * (1.0 / E) + eps_norm)
        pre = total * scale
        outs[b] = (x_own + jax.nn.silu(pre)).astype(BF16)

        @pl.when(s < S - 1)
        def _():
            remote(
                outs.at[b],
                acts.at[b, c],
                fs.at[b],
                fr.at[b],
                {"section": lax.rem(s + 1, S)},
            ).start()

        preacts[b] = pre
        scales[b] = jnp.broadcast_to(scale, (R, 128))
        rows = pl.ds(pl.multiple_of(b * R, R), R)
        normed[c, rows, :] = (x_own * scale * gain_own).astype(BF16)
        normed[1 - c, rows, :] = (x_sib * scale * gain_sib).astype(BF16)

    def features():
        for half_index in range(2):

            @pl.loop(0, H // 128)
            def _(j):
                cols = pl.ds(pl.multiple_of(j * 128, 128), 128)
                flipped = jnp.transpose(normed[half_index, :, cols].astype(F32))
                normed_t[pl.ds(pl.multiple_of(half_index * H + j * 128, 128), 128), :] = (
                    flipped.astype(BF16)
                )

        @pl.loop(1, D)
        def _(k):
            to = lax.rem(a + k, D)
            remote(
                normed_t.at[pl.ds(pl.multiple_of(to * RB, 16), RB), :],
                feats.at[:, pl.ds(pl.multiple_of(a * TOK, 128), TOK)],
                ts.at[to],
                tr.at[a],
                {"dp": to},
            ).start()

        feats[:, pl.ds(pl.multiple_of(a * TOK, 128), TOK)] = normed_t[
            pl.ds(pl.multiple_of(a * RB, 16), RB), :
        ]

    @pl.when(s < (S + 1) // 2)
    def _():
        features()

    def dpre_rows(owner, b):
        return dpres.at[pl.ds(pl.multiple_of(owner * TOK + b * R, R), R), :]

    @pl.loop(0, MB)
    def _(b):
        @pl.when(s == S - 1)
        def _():
            pltpu.make_async_copy(
                cotangent.at[b, :, pl.ds(pl.multiple_of(c * H, 128), H)],
                grads_in.at[b],
                local_sem.at[MB + b],
            ).wait()

        @pl.when(s < S - 1)
        def _():
            pltpu.make_async_copy(grads_out.at[b], grads_in.at[b], br.at[b]).wait()

        upstream = grads_in[b].astype(F32)
        pre = preacts[b]
        sig = jax.nn.sigmoid(pre)
        dpre = (upstream * (sig * (1.0 + pre * (1.0 - sig)))).astype(BF16)
        dpres[pl.ds(pl.multiple_of(a * TOK + b * R, R), R), :] = dpre

        @pl.when(s > 0)
        def _():
            stat = jnp.sum(dpre.astype(F32) * pre, axis=1, keepdims=True)
            stat_send[b] = jnp.broadcast_to(stat, (R, 128))
            remote(stat_send.at[b], stat_recv.at[b], ss.at[b], sr.at[b], sib).start()
            part_send[b] = lax.dot_general(
                dpre,
                weights[sib_rows, :],
                (((1,), (1,)), ((), ())),
                preferred_element_type=F32,
            ).astype(BF16)
            remote(part_send.at[b], part_recv.at[b], ps.at[b], pr.at[b], sib).start()
            part = lax.dot_general(
                dpre,
                weights[own_rows, :],
                (((1,), (1,)), ((), ())),
                preferred_element_type=F32,
            )
            pltpu.make_async_copy(stat_send.at[b], stat_recv.at[b], sr.at[b]).wait()
            scale = scales[b][:, :1]
            both = (stat + stat_recv[b][:, :1]) * (1.0 / E)
            pltpu.make_async_copy(part_send.at[b], part_recv.at[b], pr.at[b]).wait()
            dnormed = part + part_recv[b].astype(F32)
            back = (
                upstream
                + scale * (gain_own * dnormed)
                - acts[b, c].astype(F32) * (scale * scale * both)
            )
            grads_out[b] = back.astype(BF16)
            remote(
                grads_out.at[b],
                grads_in.at[b],
                bs.at[b],
                br.at[b],
                {"section": lax.rem(s + S - 1, S)},
            ).start()

        @pl.loop(1, D)
        def _(k):
            to = lax.rem(a + k, D)
            remote(
                dpre_rows(a, b), dpre_rows(a, b), ds.at[b, to], dr.at[b, a], {"dp": to}
            ).start()

    @pl.when(s >= (S + 1) // 2)
    def _():
        features()

    arrived(m_send, m_recv, ms, mr)
    assemble(m_recv, new_m.at[0])
    arrived(v_send, v_recv, vs, vr)
    assemble(v_recv, new_v.at[0])

    @pl.loop(1, D)
    def _(k):
        of = lax.rem(a + k, D)
        there = feats.at[:, pl.ds(pl.multiple_of(of * TOK, 128), TOK)]
        pltpu.make_async_copy(there, there, tr.at[of]).wait()

        @pl.loop(0, MB)
        def _(b):
            pltpu.make_async_copy(dpre_rows(of, b), dpre_rows(of, b), dr.at[b, of]).wait()

    fix_one = 1.0 - beta_one**step_count
    fix_two = 1.0 - beta_two**step_count

    def update(cols):
        grad = jnp.dot(feats[...], dpres[:, cols], preferred_element_type=F32)
        moment = beta_one * new_m[0, :, cols].astype(F32) + (1.0 - beta_one) * grad
        second = beta_two * new_v[0, :, cols].astype(F32) + (1.0 - beta_two) * grad * grad
        direction = moment / fix_one / (jnp.sqrt(second / fix_two) + adam_eps)
        master = block[:, cols].astype(F32)
        new_w[0, :, cols] = master - learn_rate * (direction + decay_rate * master)
        new_m[0, :, cols] = moment.astype(BF16)
        new_v[0, :, cols] = second.astype(BF16)

    @pl.loop(0, H // 256)
    def _(j):
        update(pl.ds(pl.multiple_of(j * 256, 128), 256))

    if H % 256:
        update(pl.ds(H - H % 256, H % 256))

    drained(w_send, w_recv, ws, wr)
    drained(m_send, m_recv, ms, mr)
    drained(v_send, v_recv, vs, vr)
    for cp in pending:
        cp.wait_send()

    @pl.loop(0, MB)
    def _(b):
        remote(acts.at[b, c], acts.at[b, c], rs.at[b], rr.at[b], sib).wait_send()

        @pl.when(s < S - 1)
        def _():
            remote(outs.at[b], acts.at[b, c], fs.at[b], fr.at[b], sib).wait_send()

        @pl.when(s > 0)
        def _():
            remote(stat_send.at[b], stat_recv.at[b], ss.at[b], sr.at[b], sib).wait_send()
            remote(part_send.at[b], part_recv.at[b], ps.at[b], pr.at[b], sib).wait_send()
            remote(grads_out.at[b], grads_in.at[b], bs.at[b], br.at[b], sib).wait_send()

        @pl.loop(1, D)
        def _(k):
            to = lax.rem(a + k, D)
            remote(
                dpre_rows(a, b), dpre_rows(a, b), ds.at[b, to], dr.at[b, a], {"dp": to}
            ).wait_send()

    @pl.loop(1, D)
    def _(k):
        to = lax.rem(a + k, D)
        remote(
            normed_t.at[pl.ds(pl.multiple_of(to * RB, 16), RB), :],
            feats.at[:, pl.ds(pl.multiple_of(a * TOK, 128), TOK)],
            ts.at[to],
            tr.at[a],
            {"dp": to},
        ).wait_send()


def local(old_w, old_m, old_v, old_slot_layer, norm_gain, tokens, cotangent):
    S = lax.axis_size("section")
    D = lax.axis_size("dp")
    PR, H = old_w.shape[3], old_w.shape[4]
    MB, R = tokens.shape[0], tokens.shape[1]
    RB = S * PR
    TOK = MB * R
    E = 2 * H
    layer_ids = jnp.arange(S, dtype=jnp.int32)
    matches = (old_slot_layer[None, :] == layer_ids[:, None]).astype(jnp.int32)
    order = jnp.sum(matches * layer_ids[None, :], axis=1)
    vmem = pl.BlockSpec(memory_space=pltpu.VMEM)
    anyspace = pl.BlockSpec(memory_space=pl.ANY)
    dma = pltpu.SemaphoreType.DMA
    new_w, new_m, new_v = pl.pallas_call(
        functools.partial(kernel, (S, D, PR, H, MB, R)),
        out_shape=(
            jax.ShapeDtypeStruct((1, RB, H), F32),
            jax.ShapeDtypeStruct((1, RB, H), BF16),
            jax.ShapeDtypeStruct((1, RB, H), BF16),
        ),
        in_specs=[pl.BlockSpec(memory_space=pltpu.SMEM), vmem, vmem, vmem, vmem, anyspace, anyspace],
        out_specs=(vmem, vmem, vmem),
        scratch_shapes=[
            pltpu.VMEM((S, PR, H), BF16),
            pltpu.VMEM((S, PR, H), BF16),
            pltpu.VMEM((S, PR, H), BF16),
            pltpu.VMEM((S, PR, H), BF16),
            pltpu.VMEM((S, PR, H), BF16),
            pltpu.VMEM((S, PR, H), BF16),
            pltpu.VMEM((RB, 128), F32),
            pltpu.VMEM((RB, H), BF16),
            pltpu.VMEM((E, H), BF16),
            pltpu.VMEM((MB, 2, R, H), BF16),
            pltpu.VMEM((MB, R, H), BF16),
            pltpu.VMEM((MB, R, H), F32),
            pltpu.VMEM((MB, R, 128), F32),
            pltpu.VMEM((2, TOK, H), BF16),
            pltpu.VMEM((E, TOK), BF16),
            pltpu.VMEM((RB, D * TOK), BF16),
            pltpu.VMEM((MB, R, H), BF16),
            pltpu.VMEM((MB, R, H), BF16),
            pltpu.VMEM((D * TOK, H), BF16),
            pltpu.VMEM((MB, R, H), BF16),
            pltpu.VMEM((MB, R, H), BF16),
            pltpu.VMEM((MB, R, 128), F32),
            pltpu.VMEM((MB, R, 128), F32),
            dma((S,)),
            dma((S,)),
            dma((S,)),
            dma((S,)),
            dma((S,)),
            dma((S,)),
            dma((14,)),
            dma((14,)),
            dma((MB,)),
            dma((MB,)),
            dma((MB,)),
            dma((MB,)),
            dma((MB,)),
            dma((MB,)),
            dma((MB,)),
            dma((MB,)),
            dma((MB,)),
            dma((MB,)),
            dma((D,)),
            dma((D,)),
            dma((MB, D)),
            dma((MB, D)),
            dma((2 * MB + 1,)),
        ],
        compiler_params=pltpu.CompilerParams(
            collective_id=0, has_side_effects=True, vmem_limit_bytes=63_000_000
        ),
    )(
        order,
        old_w.reshape(S, PR, H),
        old_m.reshape(S, PR, H),
        old_v.reshape(S, PR, H),
        norm_gain.reshape(2, 1, H),
        tokens,
        cotangent,
    )
    return new_w, new_m, new_v


def solution(mesh):
    placed = (
        P(None, "dp", "section", None, "mp"),
        P(None, "dp", "section", None, "mp"),
        P(None, "dp", "section", None, "mp"),
        P(),
        P("section", None),
        P(None, "dp", None),
        P(None, "dp", None),
    )
    return jax.shard_map(
        local,
        mesh=mesh,
        in_specs=placed,
        out_specs=(P("section", "dp", "mp"), P("section", "dp", "mp"), P("section", "dp", "mp")),
        check_vma=False,
    )
```

time: 1810 us -> 473 us (0.26)
  waiting for transfers between devices: 1190 us -> 0 us
  Pallas kernels: 0 us -> 458 us
  starting transfers between devices: 221 us -> 0 us
  blocking collectives: 115 us -> 0 us
  matrix products: 113 us -> 0 us
  other arithmetic: 101 us -> 1.28 us
  local copies, waits for them, and re-layouts: 39.3 us -> 12.9 us
    psum x23 -> x0, waiting for transfers between devices: 862 us -> none  [backward_tick(): lax.psum(partial_value.astype(jnp.bfloat16), 'mp').astype(jnp.float32)]
    pallas_call x0 -> x1, Pallas kernels: none -> 458 us  [local(): pl.pallas_call(functools.partial(kernel, (S, D, PR, H, MB, R)), out_shape...]
    ppermute x46 -> x0, starting transfers between devices: 202 us -> none  [from_behind(): return lax.ppermute(value, axis, pairs)]
    ppermute x46 -> x0, waiting for transfers between devices: 157 us -> none  [from_behind(): return lax.ppermute(value, axis, pairs)]
    all_gather x2 -> x0, waiting for transfers between devices: 117 us -> none  [the longest x1 117 us: local(): lax.all_gather(master.astype(jnp.bfloat16), 'dp', axis=0, tiled=True)]
    dot_general x17 -> x0, matrix products: 113 us -> none  [the longest x8 57.5 us: grad_part(): lax.dot_general(dpre, weight_copy, (((1,), (1,)), ((), ())), preferred_el...]
    all_gather x23 -> x0, blocking collectives: 62.1 us -> none  [forward_send(): joined = lax.all_gather(output, 'mp', axis=1, tiled=True)]
    all_to_all x1 -> x0, blocking collectives: 52.9 us -> none  [local(): lax.all_to_all(ordered_w.astype(jnp.bfloat16), 'section', split_axis=0, c...]
  transfers between devices with their start and end apart: 74 -> 0, of which waited for: 72 -> 0; matrix products, arithmetic and copies ran while one was open for 12% -> 0% of each run, Pallas kernels for 0% -> 0%
where the time goes in v1:
time: 473 us
  Pallas kernels  458 us (97%)
  local copies, waits for them, and re-layouts  12.9 us (3%)
    pallas_call x1, Pallas kernels, local(): pl.pallas_call(functools.partial(kernel, (S, D, PR, H, MB, R)), out_shape...  458 us

profile of v1, /device:TPU:1, one launch (start us, length us, event | category | flops | bytes accessed | tf_op | source)
XLA Modules:
  0.0 472.7 jit_solution(7783704573527764555)
XLA Ops:
  0.6 1.3 select_reduce_fusion.order
  1.9 0.0 copy-start
  1.9 0.0 copy-start.1
  1.9 4.0 copy.24
  5.9 0.0 copy-done
  5.9 0.0 copy-done.1
  5.9 2.3 copy_bitcast_fusion.1
  8.3 457.9 %shard_map.94 = (f32[1,416,1664]{2,1,0:T(8,128)}, bf16[1,416,1664]{2,1,0:T(8,128)(2,1)}, bf16[1,416,1664]{2,1,0:T(8,128)(2,1)}) custom-call(s32[16]{0:T(128)} %select_reduce_fusion.order, f32[16,26,1664]{2,1,0:T(8,128)} %bitcast.9, bf16[16,26,1664]{2,1,0:T(8,128)(2,1)} %get-tuple-element.4.old_m, bf16[16,26,1664]{2,1,0:T(8,128)(2,1)} %get-tuple-element.3.old_v, ...), custom_call_target="tpu_custom_call" | custom-call | tf_op jit(solution)/shard_map/pallas_call | solution.py:510
  466.2 0.0 copy-start.3
  466.2 3.6 copy.28
  469.8 0.0 copy-done.3
  469.8 0.0 copy-start.2
  469.8 1.1 copy.29
  470.9 0.8 copy-done.2
  471.7 1.1 copy.30
Async XLA Ops:
  1.9 4.0 copy-start
  1.9 4.0 copy-start.1
  466.2 3.6 copy-start.3
  469.8 1.8 copy-start.2

commit v2 on v1

v2 whole, which is shorter than its diff:
```python
import functools

import jax
import jax.numpy as jnp
from jax import lax
from jax.experimental import pallas as pl
from jax.experimental.pallas import tpu as pltpu
from jax.sharding import PartitionSpec as P

eps_norm = 1e-05
beta_one = 0.9
beta_two = 0.95
learn_rate = 0.001
decay_rate = 0.1
adam_eps = 1e-08
step_count = 1000.0

MESH = pl.DeviceIdType.MESH
F32 = jnp.float32
BF16 = jnp.bfloat16
XS = 4


def remote(src, dst, send_sem, recv_sem, device):
    return pltpu.make_async_remote_copy(
        src_ref=src,
        dst_ref=dst,
        send_sem=send_sem,
        recv_sem=recv_sem,
        device_id=device,
        device_id_type=MESH,
    )


def relay_plan(rows):
    two_thirds = max(16, (rows * 2 // 3 + 15) // 16 * 16)
    half = (rows // 2 + 15) // 16 * 16
    return two_thirds, half


def feature_width(rows, half):
    return max(
        -(-(rows * k % 128 + rows) // 128) * 128 for k in range(half // rows)
    )


def kernel(
    sizes,
    order,
    old_w,
    old_m,
    old_v,
    gain,
    tokens,
    cotangent,
    grad_out,
    block_out,
    m_out,
    v_out,
    w_send,
    m_send,
    v_send,
    w_recv,
    m_recv,
    v_recv,
    pick,
    wide,
    block,
    first,
    second,
    weights,
    flipped,
    acts,
    outs,
    preacts,
    scales,
    normed,
    raw_feats,
    feats,
    grads_in,
    grads_out,
    dpres,
    part_send,
    part_recv,
    stat_send,
    stat_recv,
    ws,
    wr,
    ms,
    mr,
    vs,
    vr,
    gs,
    gr,
    fs,
    fr,
    rs,
    rr,
    ps,
    pr,
    ss,
    sr,
    bs,
    br,
    ts,
    tr,
    ds,
    dr,
    local_sem,
    out_sem,
):
    S, D, pr_rows, H, MB, R = sizes
    RB = S * pr_rows
    TOK = MB * R
    E = 2 * H
    s = lax.axis_index("section")
    a = lax.axis_index("dp")
    c = lax.axis_index("mp")
    sib = {"mp": 1 - c}
    lanes = H // 128
    cut = (lanes + 1) // 2 * 128
    chunks = ((0, cut), (cut, H - cut))
    width = feature_width(RB, H)

    barrier = pltpu.get_barrier_semaphore()

    @pl.loop(1, S)
    def _(k):
        pl.semaphore_signal(
            barrier, inc=1, device_id={"section": lax.rem(s + k, S)}, device_id_type=MESH
        )

    @pl.loop(1, D)
    def _(k):
        pl.semaphore_signal(
            barrier, inc=1, device_id={"dp": lax.rem(a + k, D)}, device_id_type=MESH
        )

    pl.semaphore_signal(barrier, inc=1, device_id=sib, device_id_type=MESH)

    @pl.when(s == 0)
    def _():
        @pl.loop(0, MB)
        def _(b):
            pltpu.make_async_copy(
                tokens.at[b, :, pl.ds(pl.multiple_of(c * H, 128), H)],
                acts.at[b, c],
                local_sem.at[b],
            ).start()

    @pl.when(s == S - 1)
    def _():
        @pl.loop(0, MB)
        def _(b):
            pltpu.make_async_copy(
                cotangent.at[b, :, pl.ds(pl.multiple_of(c * H, 128), H)],
                grads_in.at[b],
                local_sem.at[MB + b],
            ).start()

    @pl.loop(0, S)
    def _(k):
        base = order[k] * (pr_rows * lanes)
        for j in range(lanes):
            w_send[k, :, 128 * j : 128 * (j + 1)] = old_w[
                pl.ds(base + j, pr_rows, stride=lanes), :
            ].astype(BF16)

    pl.semaphore_wait(barrier, S + D - 1)

    def send_piece(send, recv, send_sems, recv_sems, to):
        @pl.when(to != s)
        def _():
            remote(
                send.at[to], recv.at[s], send_sems.at[to], recv_sems.at[s], {"section": to}
            ).start()

    def arrived(send, recv, send_sems, recv_sems):
        @pl.loop(1, S)
        def _(k):
            of = lax.rem(s + k, S)
            remote(
                send.at[of], recv.at[of], send_sems.at[of], recv_sems.at[of], {"section": of}
            ).wait_recv()

    def drained(send, recv, send_sems, recv_sems):
        @pl.loop(1, S)
        def _(k):
            of = lax.rem(s + k, S)
            remote(
                send.at[of], recv.at[of], send_sems.at[of], recv_sems.at[of], {"section": of}
            ).wait_send()

    def assemble(recv, dst):
        @pl.loop(0, H // 128)
        def _(j):
            cols = pl.ds(pl.multiple_of(j * 128, 128), 128)
            for b in range(S):
                wide[pr_rows * b : pr_rows * (b + 1), :] = recv[b, 0:pr_rows, cols].astype(F32)
            dst[:, cols] = wide[...].astype(BF16)

    @pl.loop(0, S)
    def _(to):
        send_piece(w_send, w_recv, ws, wr, to)

    w_recv[s] = w_send[s]
    arrived(w_send, w_recv, ws, wr)
    assemble(w_recv, block)

    def rows_of(owner, r0, n):
        return weights.at[pl.ds(pl.multiple_of(owner * RB + r0, 16), n), :]

    def prepare():
        padded = m_send.shape[1]

        @pl.loop(0, S)
        def _(k):
            shape = (padded, pr_rows * S)
            row = lax.broadcasted_iota(jnp.int32, shape, 0)
            col = lax.broadcasted_iota(jnp.int32, shape, 1)
            hit = col == row * S + order[k]
            pick[pl.ds(pl.multiple_of(k * padded, 16), padded), :] = jnp.where(
                hit & (row < pr_rows), 1.0, 0.0
            ).astype(BF16)

        def select(old, send):
            @pl.loop(0, lanes)
            def _(j):
                cols = pl.ds(pl.multiple_of(j * 128, 128), 128)
                flat = old[:, :, cols].reshape(pr_rows * S, 128)
                send[:, :, cols] = (
                    jnp.dot(pick[...], flat, preferred_element_type=F32)
                    .astype(BF16)
                    .reshape(S, padded, 128)
                )

        select(old_m, m_send)
        select(old_v, v_send)
        m_recv[s] = m_send[s]
        v_recv[s] = v_send[s]

    own_copy = pltpu.make_async_copy(block, rows_of(a, 0, RB), local_sem.at[2 * MB])
    own_copy.start()
    pending = []
    if D == 2 * XS:
        x = lax.rem(a, XS)
        h = a // XS

        def at(dx, dh):
            hh = (1 - h) if dh else h
            return hh * XS + lax.rem(x + dx + XS, XS)

        third, half = relay_plan(RB)
        UP, DOWN, ACROSS = at(1, 0), at(-1, 0), at(0, 1)

        def start(sem, src, owner, r0, n, to):
            cp = remote(
                src, rows_of(owner, r0, n), gs.at[sem], gr.at[sem], {"dp": to}
            )
            cp.start()
            pending.append(cp)

        def relay(sem, owner, r0, n, to):
            start(sem, rows_of(owner, r0, n), owner, r0, n, to)

        def landed(sem, owner, r0, n):
            pltpu.make_async_copy(
                rows_of(owner, r0, n), rows_of(owner, r0, n), gr.at[sem]
            ).wait()

        def blk(r0, n):
            return block.at[pl.ds(r0, n), :]

        start(0, blk(third, RB - third), a, third, RB - third, ACROSS)
        start(1, blk(0, third), a, 0, third, ACROSS)
        start(2, blk(0, half), a, 0, half, UP)
        start(3, blk(half, RB - half), a, half, RB - half, DOWN)
        start(4, blk(half, RB - half), a, half, RB - half, UP)
        start(5, blk(0, half), a, 0, half, DOWN)
        prepare()
        landed(0, ACROSS, third, RB - third)
        relay(6, ACROSS, third, RB - third, UP)
        relay(7, ACROSS, third, RB - third, DOWN)
        landed(2, DOWN, 0, half)
        relay(8, DOWN, 0, half, UP)
        landed(3, UP, half, RB - half)
        relay(9, UP, half, RB - half, DOWN)
        landed(4, DOWN, half, RB - half)
        landed(5, UP, 0, half)
        relay(10, DOWN, 0, third, ACROSS)
        relay(11, UP, 0, third, ACROSS)
        landed(1, ACROSS, 0, third)
        landed(6, at(-1, 1), third, RB - third)
        landed(7, at(1, 1), third, RB - third)
        landed(10, at(-1, 1), 0, third)
        relay(12, at(-1, 1), 0, half, UP)
        landed(11, at(1, 1), 0, third)
        relay(13, at(1, 1), half, RB - half, DOWN)
        landed(8, at(2, 0), 0, half)
        landed(9, at(2, 0), half, RB - half)
        landed(12, at(2, 1), 0, half)
        landed(13, at(2, 1), half, RB - half)
    else:
        for k in range(1, D):
            to = lax.rem(a + k, D)
            cp = remote(block, rows_of(a, 0, RB), gs.at[k], gr.at[k], {"dp": to})
            cp.start()
            pending.append(cp)
        prepare()
        for k in range(1, D):
            of = lax.rem(a - k + D, D)
            pltpu.make_async_copy(rows_of(of, 0, RB), rows_of(of, 0, RB), gr.at[k]).wait()
    own_copy.wait()
    block_copy = pltpu.make_async_copy(block, block_out, out_sem.at[0])
    block_copy.start()

    early = s < (S + 1) // 2

    def flip():
        for part_index in range(2):

            @pl.loop(0, lanes * lanes)
            def _(t):
                i = pl.multiple_of(t // lanes * 128, 128)
                j = pl.multiple_of(lax.rem(t, lanes) * 128, 128)
                flipped[part_index, pl.ds(j, 128), pl.ds(i, 128)] = jnp.transpose(
                    weights[pl.ds(pl.multiple_of(part_index * H + i, 128), 128), pl.ds(j, 128)]
                )

    @pl.when(jnp.logical_not(early))
    def _():
        flip()

    gain_own = gain[c]
    gain_sib = gain[1 - c]

    def w_rows(half_index, chunk):
        at, n = chunk
        return pl.ds(pl.multiple_of(half_index * H + at, 128), n)

    @pl.loop(0, MB)
    def _(b):
        total = jnp.zeros((R, H), F32)
        square = jnp.zeros((R, 1), F32)
        own, other = [], []

        @pl.when(s == 0)
        def _():
            pltpu.make_async_copy(
                tokens.at[b, :, pl.ds(pl.multiple_of(c * H, 128), H)],
                acts.at[b, c],
                local_sem.at[b],
            ).wait()

        for q, (at, n) in enumerate(chunks):
            here = acts.at[b, c, :, pl.ds(at, n)]

            @pl.when(s > 0)
            def _():
                pltpu.make_async_copy(here, here, fr.at[b, q]).wait()

            remote(here, here, rs.at[b, q], rr.at[b, q], sib).start()
            x = acts[b, c, :, at : at + n].astype(F32)
            own.append(x)
            square = square + jnp.sum(x * x, axis=1, keepdims=True)
            total = total + jnp.dot(
                (x * gain_own[:, at : at + n]).astype(BF16),
                weights[w_rows(c, (at, n)), :],
                preferred_element_type=F32,
            )
        for q, (at, n) in enumerate(chunks):
            there = acts.at[b, 1 - c, :, pl.ds(at, n)]
            pltpu.make_async_copy(there, there, rr.at[b, q]).wait()
            x = acts[b, 1 - c, :, at : at + n].astype(F32)
            other.append(x)
            square = square + jnp.sum(x * x, axis=1, keepdims=True)
            x_gain = (x * gain_sib[:, at : at + n]).astype(BF16)
            if q == 0:
                total = total + jnp.dot(
                    x_gain, weights[w_rows(1 - c, (at, n)), :], preferred_element_type=F32
                )
        scale = lax.rsqrt(square * (1.0 / E) + eps_norm)
        for t, (to_at, to_n) in enumerate(chunks):
            pre = (
                total[:, to_at : to_at + to_n]
                + jnp.dot(
                    x_gain,
                    weights[w_rows(1 - c, chunks[1]), to_at : to_at + to_n],
                    preferred_element_type=F32,
                )
            ) * scale
            outs[b, :, to_at : to_at + to_n] = (own[t] + jax.nn.silu(pre)).astype(BF16)

            @pl.when(s < S - 1)
            def _():
                remote(
                    outs.at[b, :, pl.ds(to_at, to_n)],
                    acts.at[b, c, :, pl.ds(to_at, to_n)],
                    fs.at[b, t],
                    fr.at[b, t],
                    {"section": lax.rem(s + 1, S)},
                ).start()

            preacts[b, :, to_at : to_at + to_n] = pre
        scales[b] = jnp.broadcast_to(scale, (R, 128))
        for q, (at, n) in enumerate(chunks):
            cols = slice(at, at + n)
            normed[c, b, :, cols] = (own[q] * scale * gain_own[:, cols]).astype(BF16)
            normed[1 - c, b, :, cols] = (other[q] * scale * gain_sib[:, cols]).astype(BF16)
        for k in range(-(-S // MB)):
            to = b * -(-S // MB) + k

            @pl.when(to < S)
            def _():
                send_piece(m_send, m_recv, ms, mr, to)
                send_piece(v_send, v_recv, vs, vr, to)

    per_half = H // RB

    def window(owner):
        offset = lax.rem(owner, per_half) * RB
        return owner // per_half, pl.multiple_of(offset // 128 * 128, 128)

    def send_features():
        @pl.loop(1, D)
        def _(k):
            to = lax.rem(a + k, D)
            half_index, at = window(to)
            remote(
                normed.at[half_index, :, :, pl.ds(at, width)],
                raw_feats.at[:, a],
                ts.at[to],
                tr.at[a],
                {"dp": to},
            ).start()

        half_index, at = window(a)
        raw_feats[:, a] = normed[half_index, :, :, pl.ds(at, width)]

    send_features()

    def gather_state():
        arrived(m_send, m_recv, ms, mr)
        assemble(m_recv, first)
        pltpu.make_async_copy(first, m_out, out_sem.at[1]).start()
        arrived(v_send, v_recv, vs, vr)
        assemble(v_recv, second)
        pltpu.make_async_copy(second, v_out, out_sem.at[2]).start()

        @pl.loop(1, D)
        def _(k):
            of = lax.rem(a + k, D)
            pltpu.make_async_copy(raw_feats.at[:, of], raw_feats.at[:, of], tr.at[of]).wait()

        @pl.loop(0, MB)
        def _(b):
            for j in range(width // 128):
                feats[b, 128 * j : 128 * (j + 1), :] = jnp.transpose(
                    raw_feats[b, :, :, 128 * j : 128 * (j + 1)].reshape(D * R, 128)
                )

    @pl.when(early)
    def _():
        flip()
        gather_state()

    def dpre_rows(owner, b):
        return dpres.at[pl.ds(pl.multiple_of((b * D + owner) * R, R), R), :]

    my_rem = pl.multiple_of(lax.rem(lax.rem(a, per_half) * RB, 128), 16)

    def weight_grad(pair):
        @pl.loop(1, D)
        def _(k):
            of = lax.rem(a + k, D)
            for b in (2 * pair, 2 * pair + 1):
                pltpu.make_async_copy(dpre_rows(of, b), dpre_rows(of, b), dr.at[b, of]).wait()

        lhs = jnp.concatenate(
            [feats[2 * pair + i, pl.ds(my_rem, RB), :] for i in range(2)], axis=1
        )
        rows = pl.ds(pl.multiple_of(pair * 2 * D * R, 2 * D * R), 2 * D * R)

        def accumulate(cols):
            value = jnp.dot(lhs, dpres[rows, cols], preferred_element_type=F32)

            @pl.when(pair == 0)
            def _():
                grad_out[:, cols] = value

            @pl.when(pair > 0)
            def _():
                grad_out[:, cols] += value

        @pl.loop(0, H // 256)
        def _(j):
            accumulate(pl.ds(pl.multiple_of(j * 256, 128), 256))

        if H % 256:
            accumulate(pl.ds(H - H % 256, H % 256))

    @pl.loop(0, MB)
    def _(b):
        @pl.when(s == S - 1)
        def _():
            pltpu.make_async_copy(
                cotangent.at[b, :, pl.ds(pl.multiple_of(c * H, 128), H)],
                grads_in.at[b],
                local_sem.at[MB + b],
            ).wait()

        def take(q, at, n):
            here = grads_in.at[b, :, pl.ds(at, n)]

            @pl.when(s < S - 1)
            def _():
                pltpu.make_async_copy(here, here, br.at[b, q]).wait()

            upstream = grads_in[b, :, at : at + n].astype(F32)
            pre = preacts[b, :, at : at + n]
            sig = jax.nn.sigmoid(pre)
            dpre = (upstream * (sig * (1.0 + pre * (1.0 - sig)))).astype(BF16)
            dpres[pl.ds(pl.multiple_of((b * D + a) * R, R), R), at : at + n] = dpre
            return upstream, pre, dpre

        @pl.when(s == 0)
        def _():
            for q, (at, n) in enumerate(chunks):
                take(q, at, n)

        @pl.when(s > 0)
        def _():
            ups = []
            stat = jnp.zeros((R, 1), F32)
            for q, (at, n) in enumerate(chunks):
                upstream, pre, dpre = take(q, at, n)
                ups.append(upstream)
                stat = stat + jnp.sum(dpre.astype(F32) * pre, axis=1, keepdims=True)
                if q == 0:
                    away = jnp.dot(
                        dpre, flipped[1 - c, at : at + n, :], preferred_element_type=F32
                    )
                    home = jnp.dot(dpre, flipped[c, at : at + n, :], preferred_element_type=F32)
            stat_send[b] = jnp.broadcast_to(stat, (R, 128))
            remote(stat_send.at[b], stat_recv.at[b], ss.at[b], sr.at[b], sib).start()
            rows = slice(chunks[1][0], H)
            for t, (at, n) in enumerate(chunks):
                part_send[b, :, at : at + n] = (
                    away[:, at : at + n]
                    + jnp.dot(
                        dpre, flipped[1 - c, rows, at : at + n], preferred_element_type=F32
                    )
                ).astype(BF16)
                remote(
                    part_send.at[b, :, pl.ds(at, n)],
                    part_recv.at[b, :, pl.ds(at, n)],
                    ps.at[b, t],
                    pr.at[b, t],
                    sib,
                ).start()
            home = home + jnp.dot(dpre, flipped[c, rows, :], preferred_element_type=F32)
            pltpu.make_async_copy(stat_send.at[b], stat_recv.at[b], sr.at[b]).wait()
            scale = scales[b][:, :1]
            shrink = scale * scale * ((stat + stat_recv[b][:, :1]) * (1.0 / E))
            for t, (at, n) in enumerate(chunks):
                cols = slice(at, at + n)
                there = part_recv.at[b, :, pl.ds(at, n)]
                pltpu.make_async_copy(there, there, pr.at[b, t]).wait()
                dnormed = home[:, cols] + part_recv[b, :, cols].astype(F32)
                back = (
                    ups[t]
                    + scale * (gain_own[:, cols] * dnormed)
                    - acts[b, c, :, cols].astype(F32) * shrink
                )
                grads_out[b, :, cols] = back.astype(BF16)
                remote(
                    grads_out.at[b, :, pl.ds(at, n)],
                    grads_in.at[b, :, pl.ds(at, n)],
                    bs.at[b, t],
                    br.at[b, t],
                    {"section": lax.rem(s + S - 1, S)},
                ).start()

        @pl.loop(1, D)
        def _(k):
            to = lax.rem(a + k, D)
            remote(
                dpre_rows(a, b), dpre_rows(a, b), ds.at[b, to], dr.at[b, a], {"dp": to}
            ).start()

        @pl.when((s == 0) & (b >= 3) & (lax.rem(b, 2) == 1))
        def _():
            weight_grad((b - 3) // 2)

    @pl.when(jnp.logical_not(early))
    def _():
        gather_state()

    @pl.loop(jnp.where(s == 0, MB // 2 - 1, 0), MB // 2)
    def _(pair):
        weight_grad(pair)

    block_copy.wait()
    pltpu.make_async_copy(first, m_out, out_sem.at[1]).wait()
    pltpu.make_async_copy(second, v_out, out_sem.at[2]).wait()
    drained(w_send, w_recv, ws, wr)
    drained(m_send, m_recv, ms, mr)
    drained(v_send, v_recv, vs, vr)
    for cp in pending:
        cp.wait_send()

    @pl.loop(0, MB)
    def _(b):
        for q, (at, n) in enumerate(chunks):
            here = acts.at[b, c, :, pl.ds(at, n)]
            remote(here, here, rs.at[b, q], rr.at[b, q], sib).wait_send()

            @pl.when(s < S - 1)
            def _():
                out = outs.at[b, :, pl.ds(at, n)]
                remote(out, here, fs.at[b, q], fr.at[b, q], sib).wait_send()

            @pl.when(s > 0)
            def _():
                part = part_send.at[b, :, pl.ds(at, n)]
                remote(
                    part, part_recv.at[b, :, pl.ds(at, n)], ps.at[b, q], pr.at[b, q], sib
                ).wait_send()
                back = grads_out.at[b, :, pl.ds(at, n)]
                remote(
                    back, grads_in.at[b, :, pl.ds(at, n)], bs.at[b, q], br.at[b, q], sib
                ).wait_send()

        @pl.when(s > 0)
        def _():
            remote(stat_send.at[b], stat_recv.at[b], ss.at[b], sr.at[b], sib).wait_send()

        @pl.loop(1, D)
        def _(k):
            to = lax.rem(a + k, D)
            remote(
                dpre_rows(a, b), dpre_rows(a, b), ds.at[b, to], dr.at[b, a], {"dp": to}
            ).wait_send()

    @pl.loop(1, D)
    def _(k):
        to = lax.rem(a + k, D)
        half_index, at = window(to)
        remote(
            normed.at[half_index, :, :, pl.ds(at, width)],
            raw_feats.at[:, a],
            ts.at[to],
            tr.at[a],
            {"dp": to},
        ).wait_send()


def local(old_w, old_m, old_v, old_slot_layer, norm_gain, tokens, cotangent):
    S = lax.axis_size("section")
    D = lax.axis_size("dp")
    PR, H = old_w.shape[3], old_w.shape[4]
    MB, R = tokens.shape[0], tokens.shape[1]
    RB = S * PR
    TOK = MB * R
    E = 2 * H
    layer_ids = jnp.arange(S, dtype=jnp.int32)
    matches = (old_slot_layer[None, :] == layer_ids[:, None]).astype(jnp.int32)
    order = jnp.sum(matches * layer_ids[None, :], axis=1)
    vmem = pl.BlockSpec(memory_space=pltpu.VMEM)
    anyspace = pl.BlockSpec(memory_space=pl.ANY)
    dma = pltpu.SemaphoreType.DMA
    padded = -(-PR // 16) * 16
    width = feature_width(RB, H)
    grad, master, moment, square = pl.pallas_call(
        functools.partial(kernel, (S, D, PR, H, MB, R)),
        out_shape=(
            jax.ShapeDtypeStruct((RB, H), F32),
            jax.ShapeDtypeStruct((RB, H), BF16),
            jax.ShapeDtypeStruct((RB, H), BF16),
            jax.ShapeDtypeStruct((RB, H), BF16),
        ),
        in_specs=[pl.BlockSpec(memory_space=pltpu.SMEM), vmem, vmem, vmem, vmem, anyspace, anyspace],
        out_specs=(vmem, anyspace, anyspace, anyspace),
        scratch_shapes=[
            pltpu.VMEM((S, PR, H), BF16),
            pltpu.VMEM((S, padded, H), BF16),
            pltpu.VMEM((S, padded, H), BF16),
            pltpu.VMEM((S, PR, H), BF16),
            pltpu.VMEM((S, padded, H), BF16),
            pltpu.VMEM((S, padded, H), BF16),
            pltpu.VMEM((S * padded, PR * S), BF16),
            pltpu.VMEM((RB, 128), F32),
            pltpu.VMEM((RB, H), BF16),
            pltpu.VMEM((RB, H), BF16),
            pltpu.VMEM((RB, H), BF16),
            pltpu.VMEM((E, H), BF16),
            pltpu.VMEM((2, H, H), BF16),
            pltpu.VMEM((MB, 2, R, H), BF16),
            pltpu.VMEM((MB, R, H), BF16),
            pltpu.VMEM((MB, R, H), F32),
            pltpu.VMEM((MB, R, 128), F32),
            pltpu.VMEM((2, MB, R, H), BF16),
            pltpu.VMEM((MB, D, R, width), BF16),
            pltpu.VMEM((MB, width, D * R), BF16),
            pltpu.VMEM((MB, R, H), BF16),
            pltpu.VMEM((MB, R, H), BF16),
            pltpu.VMEM((D * TOK, H), BF16),
            pltpu.VMEM((MB, R, H), BF16),
            pltpu.VMEM((MB, R, H), BF16),
            pltpu.VMEM((MB, R, 128), F32),
            pltpu.VMEM((MB, R, 128), F32),
            dma((S,)),
            dma((S,)),
            dma((S,)),
            dma((S,)),
            dma((S,)),
            dma((S,)),
            dma((14,)),
            dma((14,)),
            dma((MB, 2)),
            dma((MB, 2)),
            dma((MB, 2)),
            dma((MB, 2)),
            dma((MB, 2)),
            dma((MB, 2)),
            dma((MB,)),
            dma((MB,)),
            dma((MB, 2)),
            dma((MB, 2)),
            dma((D,)),
            dma((D,)),
            dma((MB, D)),
            dma((MB, D)),
            dma((2 * MB + 1,)),
            dma((3,)),
        ],
        compiler_params=pltpu.CompilerParams(
            collective_id=0, has_side_effects=True, vmem_limit_bytes=63_000_000
        ),
    )(
        order,
        old_w.reshape(S * PR * H // 128, 128),
        old_m.reshape(S, PR, H).transpose(1, 0, 2),
        old_v.reshape(S, PR, H).transpose(1, 0, 2),
        norm_gain.reshape(2, 1, H),
        tokens,
        cotangent,
    )
    moment_next = beta_one * moment.astype(F32) + (1.0 - beta_one) * grad
    second_next = beta_two * square.astype(F32) + (1.0 - beta_two) * grad * grad
    fix_one = 1.0 - beta_one**step_count
    fix_two = 1.0 - beta_two**step_count
    direction = moment_next / fix_one / (jnp.sqrt(second_next / fix_two) + adam_eps)
    kept = master.astype(F32)
    updated = kept - learn_rate * (direction + decay_rate * kept)
    return updated[None], moment_next.astype(BF16)[None], second_next.astype(BF16)[None]


def solution(mesh):
    placed = (
        P(None, "dp", "section", None, "mp"),
        P(None, "dp", "section", None, "mp"),
        P(None, "dp", "section", None, "mp"),
        P(),
        P("section", None),
        P(None, "dp", None),
        P(None, "dp", None),
    )
    return jax.shard_map(
        local,
        mesh=mesh,
        in_specs=placed,
        out_specs=(P("section", "dp", "mp"), P("section", "dp", "mp"), P("section", "dp", "mp")),
        check_vma=False,
    )
```

time: 473 us -> 536 us (1.13)
  Pallas kernels: 458 us -> 527 us
  local copies, waits for them, and re-layouts: 12.9 us -> 0 us
  other arithmetic: 1.28 us -> 8.99 us
    pallas_call x1, Pallas kernels: 458 us -> 527 us  [local(): pl.pallas_call(functools.partial(kernel, (S, D, PR, H, MB, R)), out_shape...]
    broadcast_in_dim x0 -> x1, other arithmetic: none -> 7.7 us  [local(): second_next.astype(BF16)[None]]
    unnamed x11 -> x0, local copies, waits for them, and re-layouts: 6.54 us -> none
    reshape x2 -> x0, local copies, waits for them, and re-layouts: 6.35 us -> none  [the longest x1 4 us: local(): old_w.reshape(S, PR, H)]
where the time goes in v2:
time: 536 us
  Pallas kernels  527 us (98%)
  other arithmetic  8.99 us (2%)
    pallas_call x1, Pallas kernels, local(): pl.pallas_call(functools.partial(kernel, (S, D, PR, H, MB, R)), out_shape...  527 us

profile of v2, /device:TPU:1, one launch (start us, length us, event | category | flops | bytes accessed | tf_op | source)
XLA Modules:
  0.0 536.2 jit_solution(14273407069493820570)
XLA Ops:
  0.6 1.3 select_reduce_fusion.order
  1.9 526.6 %shard_map.94 = (f32[416,1664]{1,0:T(8,128)}, bf16[416,1664]{1,0:T(8,128)(2,1)}, bf16[416,1664]{1,0:T(8,128)(2,1)}, bf16[416,1664]{1,0:T(8,128)(2,1)}) custom-call(s32[16]{0:T(128)} %select_reduce_fusion.order, f32[5408,128]{1,0:T(8,128)} %bitcast.14, bf16[26,16,1664]{2,1,0:T(8,128)(2,1)} %bitcast.15, bf16[26,16,1664]{2,1,0:T(8,128)(2,1)} %bitcast.16, ...), custom_call_target="tpu_custom_call" | custom-call | tf_op jit(solution)/shard_map/pallas_call | solution.py:674
  528.5 7.7 %fusion.6 = (bf16[1,416,1664]{2,1,0:T(8,128)(2,1)}, f32[1,416,1664]{2,1,0:T(8,128)}, bf16[1,416,1664]{2,1,0:T(8,128)(2,1)}) fusion(f32[416,1664]{1,0:T(8,128)} %get-tuple-element.9, bf16[416,1664]{1,0:T(8,128)(2,1)} %get-tuple-element.10, bf16[416,1664]{1,0:T(8,128)(2,1)} %get-tuple-element.8, bf16[416,1664]{1,0:T(8,128)(2,1)} %get-tuple-element.7), kind=kLoop, calls=%fused_computation.10 | loop fusion | flops 12460032 | bytes 12460032 | tf_op jit(solution)/shard_map/broadcast_in_dim | solution.py:756

commit v3 on v2

--- a/solution.py
+++ b/solution.py
@@ -121,6 +121,12 @@
     cut = (lanes + 1) // 2 * 128
     chunks = ((0, cut), (cut, H - cut))
     width = feature_width(RB, H)
+    rounds = 2 if S % 2 == 0 and RB // 2 % 16 == 0 else 1
+    G, GR = S // rounds, RB // rounds
+    group = s // G
+    spot = lax.rem(s, G)
+    groups = [group, 1 - group][:rounds]
+    near = sorted(range(1, G), key=lambda k: min(k, G - k))
 
     barrier = pltpu.get_barrier_semaphore()
 
@@ -169,16 +175,15 @@
     pl.semaphore_wait(barrier, S + D - 1)
 
     def send_piece(send, recv, send_sems, recv_sems, to):
-        @pl.when(to != s)
-        def _():
-            remote(
-                send.at[to], recv.at[s], send_sems.at[to], recv_sems.at[s], {"section": to}
-            ).start()
-
-    def arrived(send, recv, send_sems, recv_sems):
-        @pl.loop(1, S)
-        def _(k):
-            of = lax.rem(s + k, S)
+        remote(
+            send.at[to], recv.at[s], send_sems.at[to], recv_sems.at[s], {"section": to}
+        ).start()
+
+    def peers(which, offsets):
+        return [groups[which] * G + lax.rem(spot + k, G) for k in offsets]
+
+    def arrived(send, recv, send_sems, recv_sems, which):
+        for of in peers(which, near if which == 0 else range(G)):
             remote(
                 send.at[of], recv.at[of], send_sems.at[of], recv_sems.at[of], {"section": of}
             ).wait_recv()
@@ -191,21 +196,24 @@
                 send.at[of], recv.at[of], send_sems.at[of], recv_sems.at[of], {"section": of}
             ).wait_send()
 
-    def assemble(recv, dst):
-        @pl.loop(0, H // 128)
+    def assemble(recv, dst, which):
+        base = groups[which] * G
+        rows = pl.ds(pl.multiple_of(groups[which] * GR, 16), GR)
+
+        @pl.loop(0, lanes)
         def _(j):
             cols = pl.ds(pl.multiple_of(j * 128, 128), 128)
-            for b in range(S):
-                wide[pr_rows * b : pr_rows * (b + 1), :] = recv[b, 0:pr_rows, cols].astype(F32)
-            dst[:, cols] = wide[...].astype(BF16)
-
-    @pl.loop(0, S)
-    def _(to):
-        send_piece(w_send, w_recv, ws, wr, to)
+            for i in range(G):
+                wide[pr_rows * i : pr_rows * (i + 1), :] = recv[
+                    base + i, 0:pr_rows, cols
+                ].astype(F32)
+            dst[rows, cols] = wide[...].astype(BF16)
+
+    for which in range(rounds):
+        for to in peers(which, near if which == 0 else [0] + near):
+            send_piece(w_send, w_recv, ws, wr, to)
 
     w_recv[s] = w_send[s]
-    arrived(w_send, w_recv, ws, wr)
-    assemble(w_recv, block)
 
     def rows_of(owner, r0, n):
         return weights.at[pl.ds(pl.multiple_of(owner * RB + r0, 16), n), :]
@@ -239,78 +247,123 @@
         m_recv[s] = m_send[s]
         v_recv[s] = v_send[s]
 
-    own_copy = pltpu.make_async_copy(block, rows_of(a, 0, RB), local_sem.at[2 * MB])
-    own_copy.start()
     pending = []
-    if D == 2 * XS:
+
+    def begin(which):
+        arrived(w_send, w_recv, ws, wr, which)
+        assemble(w_recv, block, which)
+        at = pl.multiple_of(groups[which] * GR, 16)
+        own = pltpu.make_async_copy(
+            block.at[pl.ds(at, GR), :], rows_of(a, at, GR), local_sem.at[2 * MB + which]
+        )
+        own.start()
+        return own
+
+    def relays(which):
         x = lax.rem(a, XS)
         h = a // XS
+        base = pl.multiple_of(groups[which] * GR, 16)
 
         def at(dx, dh):
             hh = (1 - h) if dh else h
             return hh * XS + lax.rem(x + dx + XS, XS)
 
-        third, half = relay_plan(RB)
-        UP, DOWN, ACROSS = at(1, 0), at(-1, 0), at(0, 1)
+        third, half = relay_plan(GR)
+        up, down, across = at(1, 0), at(-1, 0), at(0, 1)
 
         def start(sem, src, owner, r0, n, to):
+            sem = sem + 14 * which
             cp = remote(
-                src, rows_of(owner, r0, n), gs.at[sem], gr.at[sem], {"dp": to}
+                src, rows_of(owner, base + r0, n), gs.at[sem], gr.at[sem], {"dp": to}
             )
             cp.start()
             pending.append(cp)
 
         def relay(sem, owner, r0, n, to):
-            start(sem, rows_of(owner, r0, n), owner, r0, n, to)
+            start(sem, rows_of(owner, base + r0, n), owner, r0, n, to)
 
         def landed(sem, owner, r0, n):
-            pltpu.make_async_copy(
-                rows_of(owner, r0, n), rows_of(owner, r0, n), gr.at[sem]
-            ).wait()
+            there = rows_of(owner, base + r0, n)
+            pltpu.make_async_copy(there, there, gr.at[sem + 14 * which]).wait()
 
         def blk(r0, n):
-            return block.at[pl.ds(r0, n), :]
-
-        start(0, blk(third, RB - third), a, third, RB - third, ACROSS)
-        start(1, blk(0, third), a, 0, third, ACROSS)
-        start(2, blk(0, half), a, 0, half, UP)
-        start(3, blk(half, RB - half), a, half, RB - half, DOWN)
-        start(4, blk(half, RB - half), a, half, RB - half, UP)
-        start(5, blk(0, half), a, 0, half, DOWN)
-        prepare()
-        landed(0, ACROSS, third, RB - third)
-        relay(6, ACROSS, third, RB - third, UP)
-        relay(7, ACROSS, third, RB - third, DOWN)
-        landed(2, DOWN, 0, half)
-        relay(8, DOWN, 0, half, UP)
-        landed(3, UP, half, RB - half)
-        relay(9, UP, half, RB - half, DOWN)
-        landed(4, DOWN, half, RB - half)
-        landed(5, UP, 0, half)
-        relay(10, DOWN, 0, third, ACROSS)
-        relay(11, UP, 0, third, ACROSS)
-        landed(1, ACROSS, 0, third)
-        landed(6, at(-1, 1), third, RB - third)
-        landed(7, at(1, 1), third, RB - third)
+            return block.at[pl.ds(pl.multiple_of(base + r0, 16), n), :]
+
+        begun = begin(which)
+        start(0, blk(third, GR - third), a, third, GR - third, across)
+        start(1, blk(0, third), a, 0, third, across)
+        start(2, blk(0, half), a, 0, half, up)
+        start(3, blk(half, GR - half), a, half, GR - half, down)
+        start(4, blk(half, GR - half), a, half, GR - half, up)
+        start(5, blk(0, half), a, 0, half, down)
+        yield
+        landed(0, across, third, GR - third)
+        relay(6, across, third, GR - third, up)
+        relay(7, across, third, GR - third, down)
+        landed(2, down, 0, half)
+        relay(8, down, 0, half, up)
+        landed(3, up, half, GR - half)
+        relay(9, up, half, GR - half, down)
+        yield
+        landed(4, down, half, GR - half)
+        relay(10, down, 0, third, across)
+        landed(5, up, 0, half)
+        relay(11, up, 0, third, across)
+        yield
+        landed(1, across, 0, third)
+        landed(6, at(-1, 1), third, GR - third)
         landed(10, at(-1, 1), 0, third)
-        relay(12, at(-1, 1), 0, half, UP)
+        relay(12, at(-1, 1), 0, half, up)
+        landed(7, at(1, 1), third, GR - third)
         landed(11, at(1, 1), 0, third)
-        relay(13, at(1, 1), half, RB - half, DOWN)
+        relay(13, at(1, 1), half, GR - half, down)
+        yield
         landed(8, at(2, 0), 0, half)
-        landed(9, at(2, 0), half, RB - half)
+        landed(9, at(2, 0), half, GR - half)
         landed(12, at(2, 1), 0, half)
-        landed(13, at(2, 1), half, RB - half)
-    else:
+        landed(13, at(2, 1), half, GR - half)
+        begun.wait()
+        yield
+
+    def direct(which):
+        base = pl.multiple_of(groups[which] * GR, 16)
+        begun = begin(which)
         for k in range(1, D):
             to = lax.rem(a + k, D)
-            cp = remote(block, rows_of(a, 0, RB), gs.at[k], gr.at[k], {"dp": to})
+            sem = k + 14 * which
+            cp = remote(
+                block.at[pl.ds(base, GR), :],
+                rows_of(a, base, GR),
+                gs.at[sem],
+                gr.at[sem],
+                {"dp": to},
+            )
             cp.start()
             pending.append(cp)
-        prepare()
+        yield
         for k in range(1, D):
-            of = lax.rem(a - k + D, D)
-            pltpu.make_async_copy(rows_of(of, 0, RB), rows_of(of, 0, RB), gr.at[k]).wait()
-    own_copy.wait()
+            there = rows_of(lax.rem(a - k + D, D), base, GR)
+            pltpu.make_async_copy(there, there, gr.at[k + 14 * which]).wait()
+        begun.wait()
+        for _ in range(4):
+            yield
+
+    def moments(which, offsets):
+        for to in peers(which, offsets):
+            send_piece(m_send, m_recv, ms, mr, to)
+            send_piece(v_send, v_recv, vs, vr, to)
+
+    routes = [(relays if D == 2 * XS else direct)(which) for which in range(rounds)]
+    next(routes[0])
+    prepare()
+    moments(0, near)
+    if rounds == 1:
+        for _ in routes[0]:
+            pass
+    else:
+        for which in (0, 1, 0, 1, 0, 1, 0, 1, 1):
+            next(routes[which])
+
     block_copy = pltpu.make_async_copy(block, block_out, out_sem.at[0])
     block_copy.start()
 
@@ -327,9 +380,16 @@
                     weights[pl.ds(pl.multiple_of(part_index * H + i, 128), 128), pl.ds(j, 128)]
                 )
 
+    behind = [0] + [k for k in near if 2 * k > G]
+    ahead = [k for k in near if 2 * k <= G]
+    if rounds == 2:
+        moments(1, behind)
+
     @pl.when(jnp.logical_not(early))
     def _():
         flip()
+        if rounds == 2:
+            moments(1, ahead)
 
     gain_own = gain[c]
     gain_sib = gain[1 - c]
@@ -407,13 +467,6 @@
             cols = slice(at, at + n)
             normed[c, b, :, cols] = (own[q] * scale * gain_own[:, cols]).astype(BF16)
             normed[1 - c, b, :, cols] = (other[q] * scale * gain_sib[:, cols]).astype(BF16)
-        for k in range(-(-S // MB)):
-            to = b * -(-S // MB) + k
-
-            @pl.when(to < S)
-            def _():
-                send_piece(m_send, m_recv, ms, mr, to)
-                send_piece(v_send, v_recv, vs, vr, to)
 
     per_half = H // RB
 
@@ -440,11 +493,13 @@
     send_features()
 
     def gather_state():
-        arrived(m_send, m_recv, ms, mr)
-        assemble(m_recv, first)
+        for which in range(rounds):
+            arrived(m_send, m_recv, ms, mr, which)
+            assemble(m_recv, first, which)
         pltpu.make_async_copy(first, m_out, out_sem.at[1]).start()
-        arrived(v_send, v_recv, vs, vr)
-        assemble(v_recv, second)
+        for which in range(rounds):
+            arrived(v_send, v_recv, vs, vr, which)
+            assemble(v_recv, second, which)
         pltpu.make_async_copy(second, v_out, out_sem.at[2]).start()
 
         @pl.loop(1, D)
@@ -462,6 +517,13 @@
     @pl.when(early)
     def _():
         flip()
+        if rounds == 2:
+            moments(1, ahead)
+
+    soon = s < max(1, S // 4)
+
+    @pl.when(soon)
+    def _():
         gather_state()
 
     def dpre_rows(owner, b):
@@ -592,7 +654,7 @@
         def _():
             weight_grad((b - 3) // 2)
 
-    @pl.when(jnp.logical_not(early))
+    @pl.when(jnp.logical_not(soon))
     def _():
         gather_state()
 
@@ -670,6 +732,7 @@
     anyspace = pl.BlockSpec(memory_space=pl.ANY)
     dma = pltpu.SemaphoreType.DMA
     padded = -(-PR // 16) * 16
+    group_rows = RB // 2 if S % 2 == 0 and RB // 2 % 16 == 0 else RB
     width = feature_width(RB, H)
     grad, master, moment, square = pl.pallas_call(
         functools.partial(kernel, (S, D, PR, H, MB, R)),
@@ -689,7 +752,7 @@
             pltpu.VMEM((S, padded, H), BF16),
             pltpu.VMEM((S, padded, H), BF16),
             pltpu.VMEM((S * padded, PR * S), BF16),
-            pltpu.VMEM((RB, 128), F32),
+            pltpu.VMEM((group_rows, 128), F32),
             pltpu.VMEM((RB, H), BF16),
             pltpu.VMEM((RB, H), BF16),
             pltpu.VMEM((RB, H), BF16),
@@ -715,8 +778,8 @@
             dma((S,)),
             dma((S,)),
             dma((S,)),
-            dma((14,)),
-            dma((14,)),
+            dma((28,)),
+            dma((28,)),
             dma((MB, 2)),
             dma((MB, 2)),
             dma((MB, 2)),
@@ -731,7 +794,7 @@
             dma((D,)),
             dma((MB, D)),
             dma((MB, D)),
-            dma((2 * MB + 1,)),
+            dma((2 * MB + 2,)),
             dma((3,)),
         ],
         compiler_params=pltpu.CompilerParams(

time: 536 us -> 383 us (0.71)
  Pallas kernels: 527 us -> 374 us
    pallas_call x1, Pallas kernels: 527 us -> 374 us  [local(): pl.pallas_call(functools.partial(kernel, (S, D, PR, H, MB, R)), out_shape...]
where the time goes in v3:
time: 383 us
  Pallas kernels  374 us (98%)
  other arithmetic  8.99 us (2%)
    pallas_call x1, Pallas kernels, local(): pl.pallas_call(functools.partial(kernel, (S, D, PR, H, MB, R)), out_shape...  374 us
    broadcast_in_dim x1, other arithmetic, local(): second_next.astype(BF16)[None]  7.7 us

profile of v3, /device:TPU:1, one launch (start us, length us, event | category | flops | bytes accessed | tf_op | source)
XLA Modules:
  0.0 383.4 jit_solution(9292136505003038188)
XLA Ops:
  0.6 1.3 select_reduce_fusion.order
  1.9 373.8 %shard_map.94 = (f32[416,1664]{1,0:T(8,128)}, bf16[416,1664]{1,0:T(8,128)(2,1)}, bf16[416,1664]{1,0:T(8,128)(2,1)}, bf16[416,1664]{1,0:T(8,128)(2,1)}) custom-call(s32[16]{0:T(128)} %select_reduce_fusion.order, f32[5408,128]{1,0:T(8,128)} %bitcast.14, bf16[26,16,1664]{2,1,0:T(8,128)(2,1)} %bitcast.15, bf16[26,16,1664]{2,1,0:T(8,128)(2,1)} %bitcast.16, ...), custom_call_target="tpu_custom_call" | custom-call | tf_op jit(solution)/shard_map/pallas_call | solution.py:737
  375.7 7.7 %fusion.6 = (bf16[1,416,1664]{2,1,0:T(8,128)(2,1)}, f32[1,416,1664]{2,1,0:T(8,128)}, bf16[1,416,1664]{2,1,0:T(8,128)(2,1)}) fusion(f32[416,1664]{1,0:T(8,128)} %get-tuple-element.9, bf16[416,1664]{1,0:T(8,128)(2,1)} %get-tuple-element.10, bf16[416,1664]{1,0:T(8,128)(2,1)} %get-tuple-element.8, bf16[416,1664]{1,0:T(8,128)(2,1)} %get-tuple-element.7), kind=kLoop, calls=%fused_computation.10 | loop fusion | flops 12460032 | bytes 12460032 | tf_op jit(solution)/shard_map/broadcast_in_dim | solution.py:819

commit v4 on v3

--- a/solution.py
+++ b/solution.py
@@ -47,9 +47,9 @@
 def kernel(
     sizes,
     order,
-    old_w,
-    old_m,
-    old_v,
+    old_w_hbm,
+    old_m_hbm,
+    old_v_hbm,
     gain,
     tokens,
     cotangent,
@@ -57,6 +57,9 @@
     block_out,
     m_out,
     v_out,
+    old_w,
+    old_m,
+    old_v,
     w_send,
     m_send,
     v_send,
@@ -108,6 +111,7 @@
     dr,
     local_sem,
     out_sem,
+    in_sem,
 ):
     S, D, pr_rows, H, MB, R = sizes
     RB = S * pr_rows
@@ -144,6 +148,15 @@
 
     pl.semaphore_signal(barrier, inc=1, device_id=sib, device_id_type=MESH)
 
+    loads = [
+        pltpu.make_async_copy(src, dst, in_sem.at[i])
+        for i, (src, dst) in enumerate(
+            ((old_w_hbm, old_w), (old_m_hbm, old_m), (old_v_hbm, old_v))
+        )
+    ]
+    for load in loads:
+        load.start()
+
     @pl.when(s == 0)
     def _():
         @pl.loop(0, MB)
@@ -164,6 +177,8 @@
                 local_sem.at[MB + b],
             ).start()
 
+    loads[0].wait()
+
     @pl.loop(0, S)
     def _(k):
         base = order[k] * (pr_rows * lanes)
@@ -219,7 +234,7 @@
         return weights.at[pl.ds(pl.multiple_of(owner * RB + r0, 16), n), :]
 
     def prepare():
-        padded = m_send.shape[1]
+        padded = pick.shape[0] // S
 
         @pl.loop(0, S)
         def _(k):
@@ -239,10 +254,12 @@
                 send[:, :, cols] = (
                     jnp.dot(pick[...], flat, preferred_element_type=F32)
                     .astype(BF16)
-                    .reshape(S, padded, 128)
+                    .reshape(S, padded, 128)[:, :pr_rows]
                 )
 
+        loads[1].wait()
         select(old_m, m_send)
+        loads[2].wait()
         select(old_v, v_send)
         m_recv[s] = m_send[s]
         v_recv[s] = v_send[s]
@@ -492,15 +509,22 @@
 
     send_features()
 
-    def gather_state():
-        for which in range(rounds):
-            arrived(m_send, m_recv, ms, mr, which)
-            assemble(m_recv, first, which)
-        pltpu.make_async_copy(first, m_out, out_sem.at[1]).start()
-        for which in range(rounds):
-            arrived(v_send, v_recv, vs, vr, which)
-            assemble(v_recv, second, which)
-        pltpu.make_async_copy(second, v_out, out_sem.at[2]).start()
+    def moment_rows(recv, send, send_sems, recv_sems, dst, which):
+        arrived(send, recv, send_sems, recv_sems, which)
+        assemble(recv, dst, which)
+
+    def first_rows(which):
+        moment_rows(m_recv, m_send, ms, mr, first, which)
+
+    def second_rows(which):
+        moment_rows(v_recv, v_send, vs, vr, second, which)
+
+    first_copy = pltpu.make_async_copy(first, m_out, out_sem.at[1])
+    second_copy = pltpu.make_async_copy(second, v_out, out_sem.at[2])
+
+    def near_state():
+        first_rows(0)
+        second_rows(0)
 
         @pl.loop(1, D)
         def _(k):
@@ -519,12 +543,7 @@
         flip()
         if rounds == 2:
             moments(1, ahead)
-
-    soon = s < max(1, S // 4)
-
-    @pl.when(soon)
-    def _():
-        gather_state()
+        near_state()
 
     def dpre_rows(owner, b):
         return dpres.at[pl.ds(pl.multiple_of((b * D + owner) * R, R), R), :]
@@ -654,17 +673,37 @@
         def _():
             weight_grad((b - 3) // 2)
 
-    @pl.when(jnp.logical_not(soon))
+        @pl.when((s == 0) & (b == MB - 4))
+        def _():
+            if rounds == 2:
+                first_rows(1)
+            first_copy.start()
+
+        @pl.when((s == 0) & (b == MB - 2))
+        def _():
+            if rounds == 2:
+                second_rows(1)
+            second_copy.start()
+
+    @pl.when(jnp.logical_not(early))
     def _():
-        gather_state()
+        near_state()
+
+    @pl.when(s > 0)
+    def _():
+        if rounds == 2:
+            first_rows(1)
+            second_rows(1)
+        first_copy.start()
+        second_copy.start()
 
     @pl.loop(jnp.where(s == 0, MB // 2 - 1, 0), MB // 2)
     def _(pair):
         weight_grad(pair)
 
     block_copy.wait()
-    pltpu.make_async_copy(first, m_out, out_sem.at[1]).wait()
-    pltpu.make_async_copy(second, v_out, out_sem.at[2]).wait()
+    first_copy.wait()
+    second_copy.wait()
     drained(w_send, w_recv, ws, wr)
     drained(m_send, m_recv, ms, mr)
     drained(v_send, v_recv, vs, vr)
@@ -742,15 +781,18 @@
             jax.ShapeDtypeStruct((RB, H), BF16),
             jax.ShapeDtypeStruct((RB, H), BF16),
         ),
-        in_specs=[pl.BlockSpec(memory_space=pltpu.SMEM), vmem, vmem, vmem, vmem, anyspace, anyspace],
+        in_specs=[pl.BlockSpec(memory_space=pltpu.SMEM), anyspace, anyspace, anyspace, vmem, anyspace, anyspace],
         out_specs=(vmem, anyspace, anyspace, anyspace),
         scratch_shapes=[
+            pltpu.VMEM((S * PR * H // 128, 128), F32),
+            pltpu.VMEM((PR, S, H), BF16),
+            pltpu.VMEM((PR, S, H), BF16),
             pltpu.VMEM((S, PR, H), BF16),
-            pltpu.VMEM((S, padded, H), BF16),
-            pltpu.VMEM((S, padded, H), BF16),
             pltpu.VMEM((S, PR, H), BF16),
-            pltpu.VMEM((S, padded, H), BF16),
-            pltpu.VMEM((S, padded, H), BF16),
+            pltpu.VMEM((S, PR, H), BF16),
+            pltpu.VMEM((S, PR, H), BF16),
+            pltpu.VMEM((S, PR, H), BF16),
+            pltpu.VMEM((S, PR, H), BF16),
             pltpu.VMEM((S * padded, PR * S), BF16),
             pltpu.VMEM((group_rows, 128), F32),
             pltpu.VMEM((RB, H), BF16),
@@ -796,6 +838,7 @@
             dma((MB, D)),
             dma((2 * MB + 2,)),
             dma((3,)),
+            dma((3,)),
         ],
         compiler_params=pltpu.CompilerParams(
             collective_id=0, has_side_effects=True, vmem_limit_bytes=63_000_000

time: 383 us -> 385 us (level)
  no operation moved by 1% of the time
where the time goes in v4:
time: 385 us
  Pallas kernels  376 us (98%)
  other arithmetic  8.99 us (2%)
    pallas_call x1, Pallas kernels, local(): pl.pallas_call(functools.partial(kernel, (S, D, PR, H, MB, R)), out_shape...  376 us
    broadcast_in_dim x1, other arithmetic, local(): second_next.astype(BF16)[None]  7.7 us

profile of v4, /device:TPU:1, one launch (start us, length us, event | category | flops | bytes accessed | tf_op | source)
XLA Modules:
  0.0 385.3 jit_solution(16304123042017588392)
XLA Ops:
  0.6 1.3 select_reduce_fusion.order
  1.9 375.7 %shard_map.94 = (f32[416,1664]{1,0:T(8,128)}, bf16[416,1664]{1,0:T(8,128)(2,1)}, bf16[416,1664]{1,0:T(8,128)(2,1)}, bf16[416,1664]{1,0:T(8,128)(2,1)}) custom-call(s32[16]{0:T(128)} %select_reduce_fusion.order, f32[5408,128]{1,0:T(8,128)} %bitcast.14, bf16[26,16,1664]{2,1,0:T(8,128)(2,1)} %bitcast.15, bf16[26,16,1664]{2,1,0:T(8,128)(2,1)} %bitcast.16, ...), custom_call_target="tpu_custom_call" | custom-call | tf_op jit(solution)/shard_map/pallas_call | solution.py:776
  377.6 7.7 %fusion.6 = (bf16[1,416,1664]{2,1,0:T(8,128)(2,1)}, f32[1,416,1664]{2,1,0:T(8,128)}, bf16[1,416,1664]{2,1,0:T(8,128)(2,1)}) fusion(f32[416,1664]{1,0:T(8,128)} %get-tuple-element.9, bf16[416,1664]{1,0:T(8,128)(2,1)} %get-tuple-element.10, bf16[416,1664]{1,0:T(8,128)(2,1)} %get-tuple-element.8, bf16[416,1664]{1,0:T(8,128)(2,1)} %get-tuple-element.7), kind=kLoop, calls=%fused_computation.10 | loop fusion | flops 12460032 | bytes 12460032 | tf_op jit(solution)/shard_map/broadcast_in_dim | solution.py:862

commit v5 on v4

--- a/solution.py
+++ b/solution.py
@@ -46,7 +46,7 @@
 
 def kernel(
     sizes,
-    order,
+    slot_layer,
     old_w_hbm,
     old_m_hbm,
     old_v_hbm,
@@ -179,9 +179,15 @@
 
     loads[0].wait()
 
+    def slot_of(layer):
+        slot = jnp.int32(0)
+        for j in range(1, S):
+            slot = jnp.where(slot_layer[j] == layer, j, slot)
+        return slot
+
     @pl.loop(0, S)
     def _(k):
-        base = order[k] * (pr_rows * lanes)
+        base = slot_of(k) * (pr_rows * lanes)
         for j in range(lanes):
             w_send[k, :, 128 * j : 128 * (j + 1)] = old_w[
                 pl.ds(base + j, pr_rows, stride=lanes), :
@@ -224,8 +230,12 @@
                 ].astype(F32)
             dst[rows, cols] = wide[...].astype(BF16)
 
-    for which in range(rounds):
-        for to in peers(which, near if which == 0 else [0] + near):
+    @pl.loop(0, S)
+    def _(k):
+        to = lax.rem(k, rounds) * G + k // rounds
+
+        @pl.when(to != s)
+        def _():
             send_piece(w_send, w_recv, ws, wr, to)
 
     w_recv[s] = w_send[s]
@@ -241,7 +251,7 @@
             shape = (padded, pr_rows * S)
             row = lax.broadcasted_iota(jnp.int32, shape, 0)
             col = lax.broadcasted_iota(jnp.int32, shape, 1)
-            hit = col == row * S + order[k]
+            hit = col == row * S + slot_of(k)
             pick[pl.ds(pl.multiple_of(k * padded, 16), padded), :] = jnp.where(
                 hit & (row < pr_rows), 1.0, 0.0
             ).astype(BF16)
@@ -378,7 +388,7 @@
         for _ in routes[0]:
             pass
     else:
-        for which in (0, 1, 0, 1, 0, 1, 0, 1, 1):
+        for which in (0, 0, 1, 0, 1, 1, 1, 0, 1):
             next(routes[which])
 
     block_copy = pltpu.make_async_copy(block, block_out, out_sem.at[0])
@@ -405,8 +415,6 @@
     @pl.when(jnp.logical_not(early))
     def _():
         flip()
-        if rounds == 2:
-            moments(1, ahead)
 
     gain_own = gain[c]
     gain_sib = gain[1 - c]
@@ -541,8 +549,6 @@
     @pl.when(early)
     def _():
         flip()
-        if rounds == 2:
-            moments(1, ahead)
         near_state()
 
     def dpre_rows(owner, b):
@@ -669,6 +675,12 @@
                 dpre_rows(a, b), dpre_rows(a, b), ds.at[b, to], dr.at[b, a], {"dp": to}
             ).start()
 
+        if rounds == 2:
+
+            @pl.when(b == 0)
+            def _():
+                moments(1, ahead)
+
         @pl.when((s == 0) & (b >= 3) & (lax.rem(b, 2) == 1))
         def _():
             weight_grad((b - 3) // 2)
@@ -764,9 +776,6 @@
     RB = S * PR
     TOK = MB * R
     E = 2 * H
-    layer_ids = jnp.arange(S, dtype=jnp.int32)
-    matches = (old_slot_layer[None, :] == layer_ids[:, None]).astype(jnp.int32)
-    order = jnp.sum(matches * layer_ids[None, :], axis=1)
     vmem = pl.BlockSpec(memory_space=pltpu.VMEM)
     anyspace = pl.BlockSpec(memory_space=pl.ANY)
     dma = pltpu.SemaphoreType.DMA
@@ -844,7 +853,7 @@
             collective_id=0, has_side_effects=True, vmem_limit_bytes=63_000_000
         ),
     )(
-        order,
+        old_slot_layer,
         old_w.reshape(S * PR * H // 128, 128),
         old_m.reshape(S, PR, H).transpose(1, 0, 2),
         old_v.reshape(S, PR, H).transpose(1, 0, 2),

time: 385 us -> 377 us (0.979)
  Pallas kernels: 376 us -> 369 us
    pallas_call x1, Pallas kernels: 376 us -> 369 us  [local(): pl.pallas_call(functools.partial(kernel, (S, D, PR, H, MB, R)), out_shape...]
where the time goes in v5:
time: 377 us
  Pallas kernels  369 us (98%)
  other arithmetic  7.7 us (2%)
    pallas_call x1, Pallas kernels, local(): pl.pallas_call(functools.partial(kernel, (S, D, PR, H, MB, R)), out_shape...  369 us
    broadcast_in_dim x1, other arithmetic, local(): second_next.astype(BF16)[None]  7.7 us

profile of v5, /device:TPU:1, one launch (start us, length us, event | category | flops | bytes accessed | tf_op | source)
XLA Modules:
  0.0 377.3 jit_solution(33530728381472821)
XLA Ops:
  0.6 369.0 %shard_map.94 = (f32[416,1664]{1,0:T(8,128)}, bf16[416,1664]{1,0:T(8,128)(2,1)}, bf16[416,1664]{1,0:T(8,128)(2,1)}, bf16[416,1664]{1,0:T(8,128)(2,1)}) custom-call(s32[16]{0:T(128)} %slot_layer.1, f32[5408,128]{1,0:T(8,128)} %bitcast.14, bf16[26,16,1664]{2,1,0:T(8,128)(2,1)} %bitcast.15, bf16[26,16,1664]{2,1,0:T(8,128)(2,1)} %bitcast.16, ...), custom_call_target="tpu_custom_call" | custom-call | tf_op jit(solution)/shard_map/pallas_call | solution.py:785
  369.6 7.7 %fusion.6 = (bf16[1,416,1664]{2,1,0:T(8,128)(2,1)}, f32[1,416,1664]{2,1,0:T(8,128)}, bf16[1,416,1664]{2,1,0:T(8,128)(2,1)}) fusion(f32[416,1664]{1,0:T(8,128)} %get-tuple-element.9, bf16[416,1664]{1,0:T(8,128)(2,1)} %get-tuple-element.10, bf16[416,1664]{1,0:T(8,128)(2,1)} %get-tuple-element.8, bf16[416,1664]{1,0:T(8,128)(2,1)} %get-tuple-element.7), kind=kLoop, calls=%fused_computation.10 | loop fusion | flops 12460032 | bytes 12460032 | tf_op jit(solution)/shard_map/broadcast_in_dim | solution.py:871

commit v6 on v5

--- a/solution.py
+++ b/solution.py
@@ -549,6 +549,8 @@
     @pl.when(early)
     def _():
         flip()
+        if rounds == 2:
+            moments(1, ahead)
         near_state()
 
     def dpre_rows(owner, b):
@@ -677,7 +679,7 @@
 
         if rounds == 2:
 
-            @pl.when(b == 0)
+            @pl.when(jnp.logical_not(early) & (b == 0))
             def _():
                 moments(1, ahead)
 

time: 377 us -> 360 us (0.955)
  Pallas kernels: 369 us -> 352 us
    pallas_call x1, Pallas kernels: 369 us -> 352 us  [local(): pl.pallas_call(functools.partial(kernel, (S, D, PR, H, MB, R)), out_shape...]
where the time goes in v6:
time: 360 us
  Pallas kernels  352 us (98%)
  other arithmetic  7.7 us (2%)
    pallas_call x1, Pallas kernels, local(): pl.pallas_call(functools.partial(kernel, (S, D, PR, H, MB, R)), out_shape...  352 us
    broadcast_in_dim x1, other arithmetic, local(): second_next.astype(BF16)[None]  7.7 us

profile of v6, /device:TPU:1, one launch (start us, length us, event | category | flops | bytes accessed | tf_op | source)
XLA Modules:
  0.0 360.2 jit_solution(17668847754334567539)
XLA Ops:
  0.6 351.9 %shard_map.94 = (f32[416,1664]{1,0:T(8,128)}, bf16[416,1664]{1,0:T(8,128)(2,1)}, bf16[416,1664]{1,0:T(8,128)(2,1)}, bf16[416,1664]{1,0:T(8,128)(2,1)}) custom-call(s32[16]{0:T(128)} %slot_layer.1, f32[5408,128]{1,0:T(8,128)} %bitcast.14, bf16[26,16,1664]{2,1,0:T(8,128)(2,1)} %bitcast.15, bf16[26,16,1664]{2,1,0:T(8,128)(2,1)} %bitcast.16, ...), custom_call_target="tpu_custom_call" | custom-call | tf_op jit(solution)/shard_map/pallas_call | solution.py:787
  352.5 7.7 %fusion.6 = (bf16[1,416,1664]{2,1,0:T(8,128)(2,1)}, f32[1,416,1664]{2,1,0:T(8,128)}, bf16[1,416,1664]{2,1,0:T(8,128)(2,1)}) fusion(f32[416,1664]{1,0:T(8,128)} %get-tuple-element.9, bf16[416,1664]{1,0:T(8,128)(2,1)} %get-tuple-element.10, bf16[416,1664]{1,0:T(8,128)(2,1)} %get-tuple-element.8, bf16[416,1664]{1,0:T(8,128)(2,1)} %get-tuple-element.7), kind=kLoop, calls=%fused_computation.10 | loop fusion | flops 12460032 | bytes 12460032 | tf_op jit(solution)/shard_map/broadcast_in_dim | solution.py:873
